TPU v7x, 32 devices: a whole 2x2x4 slice. The times are simulated.
32 devices in a mesh: dp: 8 (over z, y), tensor: 4 (over x, core).
Axes of the slice: x: 2, y: 2, z: 4, core: 2. Of those that a mesh axis runs over, the one named last changes fastest.
Arguments:
- tokens: bfloat16 [16384, 768], P(('dp', 'tensor')), may hold values from -6 to 6
- memory: bfloat16 [8192, 768], P(('dp', 'tensor')), may hold values from -6 to 6
- cotangent: bfloat16 [16384, 768], P(('dp', 'tensor')), may hold values from -6 to 6
- norm_gains: float32 [3, 768], replicated, may hold values from 0.5 to 1.5
- query_weight: bfloat16 [2, 768, 768], P(None, None, 'tensor'), may hold values from -0.0546875 to 0.0546875
- keyvalue_weight: bfloat16 [2, 2, 768, 768], P(None, None, None, 'tensor'), may hold values from -0.21875 to 0.21875
- output_weight: bfloat16 [2, 768, 768], P(None, 'tensor'), may hold values from -0.625 to 0.625
- bias_table: float32 [32, 12], P(None, 'tensor'), may hold values from -5 to 5
- inner_weight: bfloat16 [2, 768, 2048], P(None, None, 'tensor'), may hold values from -0.21875 to 0.21875
- outer_weight: bfloat16 [2048, 768], P('tensor'), may hold values from -0.1875 to 0.1875
- target_lengths: int32 [16, 12], P('dp'), may hold values from 0 to 512, as said below
- source_lengths: int32 [16, 12], P('dp'), may hold values from 0 to 42, as said below
Outputs:
- output_rows: bfloat16 [16384, 768], P(('dp', 'tensor'))
- tokens_grad: float32 [16384, 768], P(('dp', 'tensor'))
- memory_grad: float32 [8192, 768], P(('dp', 'tensor'))
- gains_grad: float32 [3, 768], replicated
- query_grad: float32 [2, 768, 768], P(None, None, 'tensor')
- keyvalue_grad: float32 [2, 2, 768, 768], P(None, None, None, 'tensor')
- output_grad: float32 [2, 768, 768], P(None, 'tensor')
- table_grad: float32 [32, 12], P(None, 'tensor')
- inner_grad: float32 [2, 768, 2048], P(None, None, 'tensor')
- outer_grad: float32 [2048, 768], P('tensor')
- model_stats: float32 [11, 768], replicated
- head_stats: float32 [6, 768], P(None, 'tensor')
- projection_stats: float32 [2, 768], P(None, 'tensor')
- unit_stats: float32 [3, 2048], P(None, 'tensor')
Inputs may be any that keep to these rules, and one draw needn't show every extreme that they name: `target_lengths`: A row lists the decoder lengths of the documents packed in one slot in order; the first is 1 or more, zeros stand only after the last document, and a row sums to at most 1024. `source_lengths`: A row lists the encoder lengths of the same documents: 1 or more exactly where the decoder length is, zero elsewhere; a row sums to at most 512.
All inputs are finite; a program needn't handle non-finite values.
Results may differ from a plain program's by a relative error of at most 0.023.
The roundings to bfloat16 on the way count: a program that leaves them out, or rounds other values in their place, can miss the bound.
Values may be sent and summed in bfloat16 or wider, within the bound.
No kernel may reach another device: no remote copies, remote signals or barrier semaphores. Data moves between devices by JAX's collectives and lax.ppermute only.
A program may use at most 192 MiB of HBM per device.

v0:
```python
import math

import jax
import jax.numpy as jnp
import numpy as np
from jax import lax
from jax.sharding import PartitionSpec as P

D = 768
FF = 2048
DH = 64
BUCKETS = 32
MAXDIST = 128
SLOT = 1024
MEM = 512
HD = 768


NEG_FILL = -1e30
NORM_EPS = 1e-06


def bucket_list(position_count, buckets, max_reach):
    exact_count = buckets // 2
    chosen = []
    for spread in range(position_count):
        if spread < exact_count:
            chosen.append(spread)
        else:
            larger = exact_count + math.floor(
                math.log(spread / exact_count)
                / math.log(max_reach / exact_count)
                * (buckets - exact_count)
            )
            chosen.append(min(larger, buckets - 1))
    return np.array(chosen, dtype=np.int32)


def block_buckets(row_start, block_rows, slot_length):
    rows_here = row_start + np.arange(block_rows)
    distance = np.maximum(rows_here[:, None] - np.arange(slot_length)[None, :], 0)
    return bucket_list(slot_length, BUCKETS, MAXDIST)[distance].reshape(-1).astype(np.int32)


def block_onehot(row_start, block_rows, slot_length):
    indices = jnp.asarray(block_buckets(row_start, block_rows, slot_length))
    return (indices[:, None] == jnp.arange(BUCKETS, dtype=jnp.int32)[None, :]).astype(jnp.float32)


def block_bias(bias_table, onehot, block_rows, slot_length):
    flat_bias = lax.dot_general(
        bias_table,
        onehot,
        (((0,), (1,)), ((), ())),
        precision=lax.Precision.HIGHEST,
        preferred_element_type=jnp.float32,
    )
    return flat_bias.reshape(bias_table.shape[1], block_rows, slot_length)


def segment_ids(lengths_row, position_count):
    ends = jnp.cumsum(lengths_row)
    places = jnp.arange(position_count, dtype=jnp.int32)
    passed = jnp.sum((places[:, None] >= ends[None, :]).astype(jnp.int32), axis=1)
    return jnp.where(places < ends[-1], passed + 1, 0)


def rms_normed(rows_in, gain_row):
    inverse_rms = lax.rsqrt(jnp.mean(rows_in * rows_in, axis=-1, keepdims=True) + NORM_EPS)
    return rows_in * inverse_rms * gain_row


def dot_rows(left_side, right_side):
    return lax.dot_general(
        left_side, right_side, (((0,), (0,)), ((), ())), preferred_element_type=jnp.float32
    )


def dot_cols(left_side, right_side):
    return lax.dot_general(
        left_side, right_side, (((1,), (1,)), ((), ())), preferred_element_type=jnp.float32
    )


def block_mask(target_seg, source_seg, row_start, block_rows, causal):
    row_seg = target_seg[row_start : row_start + block_rows]
    allowed = (row_seg[:, None] == source_seg[None, :]) & (row_seg[:, None] > 0)
    if causal:
        places = row_start + jnp.arange(block_rows)
        allowed = allowed & (places[:, None] >= jnp.arange(source_seg.shape[0])[None, :])
    return (allowed, row_seg > 0)


def block_scores(query_rows, split_key, bias_rows, allowed, head_count):
    split_query = query_rows.reshape(query_rows.shape[0], head_count, -1)
    scores = jnp.einsum("qhd,khd->hqk", split_query, split_key, preferred_element_type=jnp.float32)
    if bias_rows is not None:
        scores = scores + bias_rows
    return (jnp.where(allowed[None], scores, NEG_FILL), split_query)


def attend_slot(
    queries, keys_all, values_all, bias_table, target_seg, source_seg, causal, head_count
):
    slot_length = queries.shape[0]
    key_length = keys_all.shape[0]
    block_rows = min(512, slot_length)
    split_key = keys_all.reshape(key_length, head_count, -1)
    split_value = values_all.reshape(key_length, head_count, -1)
    contexts = []
    log_sums = []
    for row_start in range(0, slot_length, block_rows):
        allowed, live_rows = block_mask(target_seg, source_seg, row_start, block_rows, causal)
        bias_rows = None
        if bias_table is not None:
            bias_rows = block_bias(
                bias_table, block_onehot(row_start, block_rows, key_length), block_rows, key_length
            )
        masked = block_scores(
            queries[row_start : row_start + block_rows], split_key, bias_rows, allowed, head_count
        )[0]
        row_peak = jnp.max(masked, axis=-1, keepdims=True)
        exponent = jnp.exp(masked - row_peak)
        row_total = jnp.sum(exponent, axis=-1, keepdims=True)
        softmax_rows = (exponent / row_total).astype(jnp.bfloat16)
        context = jnp.einsum(
            "hqk,khd->qhd", softmax_rows, split_value, preferred_element_type=jnp.float32
        )
        context = context * live_rows[:, None, None].astype(jnp.float32)
        contexts.append(context.reshape(block_rows, -1).astype(jnp.bfloat16))
        log_sums.append((row_peak + jnp.log(row_total))[:, :, 0])
    return (jnp.concatenate(contexts, axis=0), jnp.concatenate(log_sums, axis=1))


def attend_slot_back(
    queries,
    keys_all,
    values_all,
    bias_table,
    target_seg,
    source_seg,
    causal,
    head_count,
    log_sums,
    context_grad,
):
    slot_length = queries.shape[0]
    key_length = keys_all.shape[0]
    block_rows = min(512, slot_length)
    split_key = keys_all.reshape(key_length, head_count, -1)
    split_value = values_all.reshape(key_length, head_count, -1)
    key_grad = jnp.zeros(split_key.shape, jnp.float32)
    value_grad = jnp.zeros(split_value.shape, jnp.float32)
    bucket_sum = None if bias_table is None else jnp.zeros(bias_table.shape, jnp.float32)
    query_parts = []
    for row_start in range(0, slot_length, block_rows):
        allowed, live_rows = block_mask(target_seg, source_seg, row_start, block_rows, causal)
        bias_rows = None
        onehot = None
        if bias_table is not None:
            onehot = block_onehot(row_start, block_rows, key_length)
            bias_rows = block_bias(bias_table, onehot, block_rows, key_length)
        masked, split_query = block_scores(
            queries[row_start : row_start + block_rows], split_key, bias_rows, allowed, head_count
        )
        softmax_rows = jnp.exp(masked - log_sums[:, row_start : row_start + block_rows, None])
        grad_rows = context_grad[row_start : row_start + block_rows].reshape(
            block_rows, head_count, -1
        )
        grad_rows = grad_rows * live_rows[:, None, None].astype(jnp.bfloat16)
        weight_grad = jnp.einsum(
            "qhd,khd->hqk", grad_rows, split_value, preferred_element_type=jnp.float32
        )
        value_grad = value_grad + jnp.einsum(
            "hqk,qhd->khd",
            softmax_rows.astype(jnp.bfloat16),
            grad_rows,
            preferred_element_type=jnp.float32,
        )
        inner_sum = jnp.sum(softmax_rows * weight_grad, axis=-1, keepdims=True)
        score_grad = (softmax_rows * (weight_grad - inner_sum)).astype(jnp.bfloat16)
        query_rows = jnp.einsum(
            "hqk,khd->qhd", score_grad, split_key, preferred_element_type=jnp.float32
        )
        query_parts.append(query_rows.reshape(block_rows, -1).astype(jnp.bfloat16))
        key_grad = key_grad + jnp.einsum(
            "hqk,qhd->khd", score_grad, split_query, preferred_element_type=jnp.float32
        )
        if bias_table is not None:
            flat_grad = score_grad.reshape(head_count, block_rows * key_length).astype(jnp.float32)
            bucket_sum = bucket_sum + lax.dot_general(
                onehot,
                flat_grad,
                (((0,), (1,)), ((), ())),
                precision=lax.Precision.HIGHEST,
                preferred_element_type=jnp.float32,
            )
    query_grad = jnp.concatenate(query_parts, axis=0)
    flat_key = key_grad.reshape(key_grad.shape[0], -1).astype(jnp.bfloat16)
    flat_value = value_grad.reshape(value_grad.shape[0], -1).astype(jnp.bfloat16)
    return (query_grad, flat_key, flat_value, bucket_sum)


def attend_all(
    queries, keys_all, values_all, bias_table, target_seg, source_seg, causal, head_count
):

    def one_slot(slot_parts):
        return attend_slot(
            slot_parts[0],
            slot_parts[1],
            slot_parts[2],
            bias_table,
            slot_parts[3],
            slot_parts[4],
            causal,
            head_count,
        )

    return lax.map(one_slot, (queries, keys_all, values_all, target_seg, source_seg))


def attend_back(
    queries,
    keys_all,
    values_all,
    bias_table,
    target_seg,
    source_seg,
    causal,
    head_count,
    log_sums,
    context_grad,
):

    def one_slot(bias_sum, slot_parts):
        results = attend_slot_back(
            slot_parts[0],
            slot_parts[1],
            slot_parts[2],
            bias_table,
            slot_parts[3],
            slot_parts[4],
            causal,
            head_count,
            slot_parts[5],
            slot_parts[6],
        )
        if bias_table is None:
            return (bias_sum, results[:3])
        return (bias_sum + results[3], results[:3])

    start_sum = (
        jnp.zeros((), jnp.float32)
        if bias_table is None
        else jnp.zeros(bias_table.shape, jnp.float32)
    )
    return lax.scan(
        one_slot,
        start_sum,
        (queries, keys_all, values_all, target_seg, source_seg, log_sums, context_grad),
    )


def project_in(normed, weight_cat):
    gathered = lax.all_gather(normed, "tensor", axis=0, tiled=True)
    return (gathered, jnp.dot(gathered, weight_cat, preferred_element_type=jnp.float32))


def project_out(inputs_all, weight):
    part_rows = lax.dynamic_slice_in_dim(
        inputs_all,
        jnp.int32(0),
        inputs_all.shape[0] // lax.axis_size("tensor") * lax.axis_size("tensor"),
        0,
    )
    return lax.psum_scatter(
        jnp.dot(part_rows, weight, preferred_element_type=jnp.float32),
        "tensor",
        scatter_dimension=0,
        tiled=True,
    )


def gather_grads(grad_rows):
    return lax.all_gather(grad_rows, "tensor", axis=0, tiled=True)


def scatter_grads(grads_all, weight_cat):
    part_rows = lax.dynamic_slice_in_dim(
        grads_all,
        jnp.int32(0),
        grads_all.shape[0] // lax.axis_size("tensor") * lax.axis_size("tensor"),
        0,
    )
    return lax.psum_scatter(
        dot_cols(part_rows, weight_cat), "tensor", scatter_dimension=0, tiled=True
    )


def gated_unit(gate_in, up_in):
    return jax.nn.gelu(gate_in, approximate=True) * up_in


def on_device(
    tokens,
    memory,
    cotangent,
    norm_gains,
    query_weight,
    keyvalue_weight,
    output_weight,
    bias_table,
    inner_weight,
    outer_weight,
    target_lengths,
    source_lengths,
):
    head_width = query_weight.shape[2]
    head_count = head_width // DH
    slot_count = target_lengths.shape[0]
    target_seg = jax.vmap(lambda length_row: segment_ids(length_row, SLOT))(target_lengths)
    source_seg = jax.vmap(lambda length_row: segment_ids(length_row, MEM))(source_lengths)

    def per_slot(rows_all, slot_length):
        return rows_all.reshape(slot_count, slot_length, rows_all.shape[1])

    residual = tokens.astype(jnp.float32)
    normed_first = rms_normed(residual, norm_gains[0]).astype(jnp.bfloat16)
    self_cat = jnp.concatenate(
        (query_weight[0], keyvalue_weight[0, 0], keyvalue_weight[0, 1]), axis=1
    )
    first_rows, self_proj = project_in(normed_first, self_cat)
    self_query = per_slot(self_proj[:, :head_width].astype(jnp.bfloat16), SLOT)
    self_key = per_slot(self_proj[:, head_width : 2 * head_width].astype(jnp.bfloat16), SLOT)
    self_value = per_slot(self_proj[:, 2 * head_width :].astype(jnp.bfloat16), SLOT)
    self_context, self_sums = attend_all(
        self_query, self_key, self_value, bias_table, target_seg, target_seg, True, head_count
    )
    self_flat = self_context.reshape(-1, head_width)
    after_self = residual + project_out(self_flat, output_weight[0])
    normed_second = rms_normed(after_self, norm_gains[1]).astype(jnp.bfloat16)
    second_rows, cross_proj = project_in(normed_second, query_weight[1])
    memory_all = lax.all_gather(memory, "tensor", axis=0, tiled=True)
    memory_cat = jnp.concatenate((keyvalue_weight[1, 0], keyvalue_weight[1, 1]), axis=1)
    memory_proj = jnp.dot(memory_all, memory_cat, preferred_element_type=jnp.float32)
    cross_query = per_slot(cross_proj.astype(jnp.bfloat16), SLOT)
    cross_key = per_slot(memory_proj[:, :head_width].astype(jnp.bfloat16), MEM)
    cross_value = per_slot(memory_proj[:, head_width:].astype(jnp.bfloat16), MEM)
    cross_context, cross_sums = attend_all(
        cross_query, cross_key, cross_value, None, target_seg, source_seg, False, head_count
    )
    cross_flat = cross_context.reshape(-1, head_width)
    after_cross = after_self + project_out(cross_flat, output_weight[1])
    normed_third = rms_normed(after_cross, norm_gains[2]).astype(jnp.bfloat16)
    unit_width = inner_weight.shape[2]
    inner_cat = jnp.concatenate((inner_weight[0], inner_weight[1]), axis=1)
    third_rows, gate_up = project_in(normed_third, inner_cat)
    gate_part = gate_up[:, :unit_width]
    up_part = gate_up[:, unit_width:]
    hidden = gated_unit(gate_part, up_part).astype(jnp.bfloat16)
    output_rows = after_cross + project_out(hidden, outer_weight)
    grad_after = cotangent.astype(jnp.float32)
    gelu_back = jax.vjp(gated_unit, gate_part, up_part)[1]
    branch_all = gather_grads(cotangent)
    outer_grad = dot_rows(hidden, branch_all)
    hidden_grad = dot_cols(branch_all, outer_weight)
    gate_grad, up_grad = gelu_back(hidden_grad)
    gate_up_grad = jnp.concatenate((gate_grad, up_grad), axis=1).astype(jnp.bfloat16)
    inner_both = dot_rows(third_rows, gate_up_grad)
    inner_grad = jnp.stack((inner_both[:, :unit_width], inner_both[:, unit_width:]))
    third_grad = scatter_grads(gate_up_grad, inner_cat)
    third_back = jax.vjp(rms_normed, after_cross, norm_gains[2])[1]
    residual_part, gain_third = third_back(third_grad)
    grad_after = grad_after + residual_part
    branch_all = gather_grads(grad_after.astype(jnp.bfloat16))
    cross_out_grad = dot_rows(cross_flat, branch_all)
    cross_context_grad = per_slot(dot_cols(branch_all, output_weight[1]).astype(jnp.bfloat16), SLOT)
    cross_grads = attend_back(
        cross_query,
        cross_key,
        cross_value,
        None,
        target_seg,
        source_seg,
        False,
        head_count,
        cross_sums,
        cross_context_grad,
    )[1]
    cross_query_grad = cross_grads[0].reshape(-1, head_width)
    memory_grads = jnp.concatenate(
        (cross_grads[1].reshape(-1, head_width), cross_grads[2].reshape(-1, head_width)), axis=1
    )
    cross_query_weight_grad = dot_rows(second_rows, cross_query_grad)
    memory_weight_grad = dot_rows(memory_all, memory_grads)
    part_rows = lax.slice_in_dim(memory_grads, 0, memory.shape[0] * lax.axis_size("tensor"), axis=0)
    memory_grad = lax.psum_scatter(
        dot_cols(part_rows, memory_cat), "tensor", scatter_dimension=0, tiled=True
    )
    second_back = jax.vjp(rms_normed, after_self, norm_gains[1])[1]
    residual_part, gain_second = second_back(scatter_grads(cross_query_grad, query_weight[1]))
    grad_after = grad_after + residual_part
    branch_all = gather_grads(grad_after.astype(jnp.bfloat16))
    self_out_grad = dot_rows(self_flat, branch_all)
    self_context_grad = per_slot(dot_cols(branch_all, output_weight[0]).astype(jnp.bfloat16), SLOT)
    table_grad, self_grads = attend_back(
        self_query,
        self_key,
        self_value,
        bias_table,
        target_seg,
        target_seg,
        True,
        head_count,
        self_sums,
        self_context_grad,
    )
    self_grad_cat = jnp.concatenate(
        (
            self_grads[0].reshape(-1, head_width),
            self_grads[1].reshape(-1, head_width),
            self_grads[2].reshape(-1, head_width),
        ),
        axis=1,
    )
    self_weight_grad = dot_rows(first_rows, self_grad_cat)
    first_back = jax.vjp(rms_normed, residual, norm_gains[0])[1]
    residual_part, gain_first = first_back(scatter_grads(self_grad_cat, self_cat))
    tokens_grad = grad_after + residual_part
    query_grad = jnp.stack((self_weight_grad[:, :head_width], cross_query_weight_grad))
    keyvalue_grad = jnp.stack(
        (
            jnp.stack(
                (
                    self_weight_grad[:, head_width : 2 * head_width],
                    self_weight_grad[:, 2 * head_width :],
                )
            ),
            jnp.stack((memory_weight_grad[:, :head_width], memory_weight_grad[:, head_width:])),
        )
    )
    output_grad = jnp.stack((self_out_grad, cross_out_grad))
    summed = tuple(
        lax.psum(
            (
                query_grad,
                keyvalue_grad,
                output_grad,
                table_grad,
                inner_grad,
                outer_grad,
                jnp.stack((gain_first, gain_second, gain_third)),
            ),
            "dp",
        )
    )
    query_sum, keyvalue_sum, output_sum, table_sum, inner_sum, outer_sum, gains_local = summed
    query_sq = query_sum * query_sum
    keyvalue_sq = keyvalue_sum * keyvalue_sum
    output_sq = output_sum * output_sum
    inner_sq = inner_sum * inner_sum
    outer_sq = outer_sum * outer_sum
    model_part = jnp.concatenate(
        (
            jnp.sum(query_sq, axis=2),
            jnp.sum(keyvalue_sq, axis=3).reshape(4, -1),
            jnp.sum(inner_sq, axis=2),
            jnp.sum(output_sq, axis=1),
            jnp.sum(outer_sq, axis=0)[None],
        ),
        axis=0,
    )
    gains_total, model_total = lax.psum((gains_local, model_part), "tensor")
    divisors = jnp.array([HD] * 6 + [FF] * 2 + [HD] * 2 + [FF], jnp.float32)
    model_stats = model_total / divisors[:, None]
    head_stats = (
        jnp.concatenate(
            (jnp.sum(query_sq, axis=1), jnp.sum(keyvalue_sq, axis=2).reshape(4, -1)), axis=0
        )
        / D
    )
    projection_stats = jnp.sum(output_sq, axis=2) / D
    unit_stats = (
        jnp.concatenate((jnp.sum(inner_sq, axis=1), jnp.sum(outer_sq, axis=1)[None]), axis=0) / D
    )
    return (
        output_rows.astype(jnp.bfloat16),
        tokens_grad,
        memory_grad,
        gains_total,
        query_sum,
        keyvalue_sum,
        output_sum,
        table_sum,
        inner_sum,
        outer_sum,
        model_stats,
        head_stats,
        projection_stats,
        unit_stats,
    )


def solution(mesh):
    in_specs = (
        P(("dp", "tensor"), None),
        P(("dp", "tensor"), None),
        P(("dp", "tensor"), None),
        P(),
        P(None, None, "tensor"),
        P(None, None, None, "tensor"),
        P(None, "tensor", None),
        P(None, "tensor"),
        P(None, None, "tensor"),
        P("tensor", None),
        P("dp", None),
        P("dp", None),
    )
    out_specs = (
        P(("dp", "tensor"), None),
        P(("dp", "tensor"), None),
        P(("dp", "tensor"), None),
        P(),
        P(None, None, "tensor"),
        P(None, None, None, "tensor"),
        P(None, "tensor", None),
        P(None, "tensor"),
        P(None, None, "tensor"),
        P("tensor", None),
        P(),
        P(None, "tensor"),
        P(None, "tensor"),
        P(None, "tensor"),
    )
    return jax.shard_map(
        on_device, mesh=mesh, in_specs=in_specs, out_specs=out_specs, check_vma=False
    )
```

profile of v0, /device:TPU:0, one launch (start us, length us, event | category | flops | bytes accessed | tf_op | source)
XLA Modules:
  0.0 1466.6 jit_solution(18219984139049632407)
XLA Ops:
  15.5 29.6 %all-gather.8.cloned.1.call-done = bf16[2048,768]{1,0:T(8,128)(2,1)} async-done(((bf16[512,768]{1,0:T(8,128)(2,1)}), bf16[2048,768]{1,0:T(8,128)(2,1)}) %all-gather.8.cloned.1.call-update) | async-done | bytes 3145744 | tf_op jit(solution)/shard_map/all_gather | solution.py:266
  50.4 147.3 %while.59 = (s32[]{:T(128)}, bf16[2,1024,192]{1,2,0:T(8,128)(2,1)}, f32[2,3,1024]{2,1,0:T(4,128)S(1)}, bf16[2,1024,192]{1,2,0:T(8,128)(2,1)S(1)}, s32[2,1024]{1,...) while((s32[]{:T(128)}, bf16[2,1024,192]{1,2,0:T(8,128)(2,1)}, ...), condition=%wide.region_8.9_spmd.clone, body=%wide.region_3.0_spmd.sunk.clone.sunk | while | flops 2077362688 | bytes 97954848 | solution.py:220
  71.4 20.9 %fusion.406 = f32[524288,3]{0,1:T(4,128)S(1)} fusion(f32[32,3]{0,1:T(4,128)S(1)} %get-tuple-element.1230, s32[524288]{0:T(1024)S(1)} %copy-done.115), kind=kOutput, calls=%fused_computation.85.clone.1 | convolution fusion | flops 620756992 | bytes 8388992 | tf_op jit(solution)/shard_map/while/body/eval_jaxpr/dot_general | solution.py:51
  92.4 4.7 fusion.407
  100.3 20.9 %fusion.400 = f32[524288,3]{0,1:T(4,128)S(1)} fusion(f32[32,3]{0,1:T(4,128)S(1)} %get-tuple-element.1230, s32[524288]{0:T(1024)S(1)} %copy-done.118), kind=kOutput, calls=%fused_computation.86.clone.1 | convolution fusion | flops 620756992 | bytes 8388992 | tf_op jit(solution)/shard_map/while/body/eval_jaxpr/dot_general | solution.py:51
  121.3 4.7 fusion.403
  131.8 20.9 %fusion.406 = f32[524288,3]{0,1:T(4,128)S(1)} fusion(f32[32,3]{0,1:T(4,128)S(1)} %get-tuple-element.1230, s32[524288]{0:T(1024)S(1)} %copy-done.115), kind=kOutput, calls=%fused_computation.85.clone.1 | convolution fusion | flops 620756992 | bytes 8388992 | tf_op jit(solution)/shard_map/while/body/eval_jaxpr/dot_general | solution.py:51
  152.8 4.7 fusion.407
  160.7 20.9 %fusion.400 = f32[524288,3]{0,1:T(4,128)S(1)} fusion(f32[32,3]{0,1:T(4,128)S(1)} %get-tuple-element.1230, s32[524288]{0:T(1024)S(1)} %copy-done.118), kind=kOutput, calls=%fused_computation.86.clone.1 | convolution fusion | flops 620756992 | bytes 8388992 | tf_op jit(solution)/shard_map/while/body/eval_jaxpr/dot_general | solution.py:51
  181.7 4.7 fusion.403
  205.9 57.7 %reduce-scatter.8.cloned.1.call-done = f32[512,768]{1,0:T(8,128)} async-done(((f32[2048,768]{1,0:T(8,128)}), f32[512,768]{1,0:T(8,128)}) %reduce-scatter.8.cloned.1.call-update) | async-done | bytes 1572880 | tf_op jit(solution)/shard_map/reduce_scatter | solution.py:277
  267.2 17.8 %all-gather.10.cloned.1.call-done = bf16[1024,768]{1,0:T(8,128)(2,1)} async-done(((bf16[256,768]{1,0:T(8,128)(2,1)}), bf16[1024,768]{1,0:T(8,128)(2,1)}) %all-gather.10.cloned.1.call-update) | async-done | bytes 1572880 | tf_op jit(solution)/shard_map/all_gather | solution.py:344
  288.2 27.4 %all-gather.12.cloned.1.call-done = bf16[2048,768]{1,0:T(8,128)(2,1)} async-done(((bf16[512,768]{1,0:T(8,128)(2,1)}), bf16[2048,768]{1,0:T(8,128)(2,1)}) %all-gather.12.cloned.1.call-update) | async-done | bytes 3145744 | tf_op jit(solution)/shard_map/all_gather | solution.py:266
  320.4 15.6 %while.57 = (s32[]{:T(128)}, bf16[2,1024,192]{1,2,0:T(8,128)(2,1)}, f32[2,3,1024]{2,1,0:T(4,128)}, bf16[2,512,192]{1,2,0:T(8,128)(2,1)S(1)}, s32[2,1024]{1,0:T(2...) while((s32[]{:T(128)}, bf16[2,1024,192]{1,2,0:T(8,128)(2,1)}, ...), condition=%wide.region_18.19_spmd, body=%wide.region_13.18_spmd.sunk | while | flops 419039232 | bytes 31555852 | solution.py:220
  342.8 58.5 %reduce-scatter.10.cloned.1.call-done = f32[512,768]{1,0:T(8,128)} async-done(((f32[2048,768]{1,0:T(8,128)}), f32[512,768]{1,0:T(8,128)}) %reduce-scatter.10.cloned.1.call-update) | async-done | bytes 1572880 | tf_op jit(solution)/shard_map/reduce_scatter | solution.py:277
  408.9 25.1 %all-gather.14.cloned.1.call-done = bf16[2048,768]{1,0:T(8,128)(2,1)} async-done(((bf16[512,768]{1,0:T(8,128)(2,1)}), bf16[2048,768]{1,0:T(8,128)(2,1)}) %all-gather.14.cloned.1.call-update) | async-done | bytes 3145744 | tf_op jit(solution)/shard_map/all_gather | solution.py:266
  433.9 9.1 fusion.121
  443.1 21.0 %all-gather.16.cloned.1.call-done = bf16[2048,768]{1,0:T(8,128)(2,1)} async-done(((bf16[512,768]{1,0:T(8,128)(2,1)}), bf16[2048,768]{1,0:T(8,128)(2,1)}) %all-gather.16.cloned.1.call-update) | async-done | bytes 3145744 | tf_op jit(solution)/shard_map/all_gather | solution.py:286
  464.1 8.6 fusion.108
  474.7 5.4 fusion.110
  480.2 58.5 %reduce-scatter.14.cloned.1.call-done = f32[512,768]{1,0:T(8,128)} async-done(((f32[2048,768]{1,0:T(8,128)}), f32[512,768]{1,0:T(8,128)}) %reduce-scatter.14.cloned.1.call-update) | async-done | bytes 1572880 | tf_op jit(solution)/shard_map/reduce_scatter | solution.py:296
  545.3 28.2 %all-gather.18.cloned.1.call-done = bf16[2048,768]{1,0:T(8,128)(2,1)} async-done(((bf16[512,768]{1,0:T(8,128)(2,1)}), bf16[2048,768]{1,0:T(8,128)(2,1)}) %all-gather.18.cloned.1.call-update) | async-done | bytes 3145744 | tf_op jit(solution)/shard_map/all_gather | solution.py:286
  578.5 28.4 %while.58 = (s32[]{:T(128)}, bf16[2,1024,192]{1,2,0:T(8,128)(2,1)}, bf16[2,512,192]{1,2,0:T(8,128)(2,1)}, bf16[2,512,192]{1,2,0:T(8,128)(2,1)}, bf16[2,512,192]{...) while((s32[]{:T(128)}, bf16[2,1024,192]{1,2,0:T(8,128)(2,1)}, ...), condition=%wide.region_27.28_spmd, body=%wide.region_24.27_spmd.sunk | while | flops 1028324352 | bytes 71051616 | solution.py:258
  608.1 4.7 fusion.127
  612.9 6.5 fusion.172
  619.7 51.6 %reduce-scatter.16.cloned.1.call-done = f32[512,768]{1,0:T(8,128)} async-done(((f32[2048,768]{1,0:T(8,128)}), f32[512,768]{1,0:T(8,128)}) %reduce-scatter.16.cloned.1.call-update) | async-done | bytes 1572880 | tf_op jit(solution)/shard_map/reduce_scatter | solution.py:296
  673.8 58.5 %reduce-scatter.12.cloned.1.call-done = f32[512,768]{1,0:T(8,128)} async-done(((f32[2048,768]{1,0:T(8,128)}), f32[512,768]{1,0:T(8,128)}) %reduce-scatter.12.cloned.1.call-update) | async-done | bytes 1572880 | tf_op jit(solution)/shard_map/reduce_scatter | solution.py:277
  732.3 5.3 fusion.160
  737.7 6.6 fusion.109
  759.7 6.7 all-gather.20.cloned.1.call-done
  772.4 248.9 %while.60 = (s32[]{:T(128)}, f32[32,3]{0,1:T(4,128)}, bf16[2,1024,192]{1,2,0:T(8,128)(2,1)}, bf16[2,1024,192]{1,2,0:T(8,128)(2,1)}, bf16[2,1024,192]{1,2,0:T(8,1...) while((s32[]{:T(128)}, f32[32,3]{0,1:T(4,128)}, ...), condition=%wide.region_33.34_spmd.clone.clone, body=%wide.region_30.33_spmd.sunk.clone.clone.sunk | while | flops 3524329216 | bytes 265629552 | solution.py:258
  783.6 22.5 %fusion.444 = f32[524288,3]{0,1:T(4,128)} fusion(f32[32,3]{0,1:T(4,128)} %get-tuple-element.1353, s32[524288]{0:T(1024)S(1)} %copy-done.116), kind=kOutput, calls=%fused_computation.129.clone.1 | convolution fusion | flops 620756992 | bytes 8388992 | tf_op jit(solution)/shard_map/while/body/eval_jaxpr/dot_general | solution.py:51
  806.1 9.0 multiply_reduce_fusion.27
  821.4 4.7 copy.260
  826.1 21.9 %fusion.439 = f32[524288,3]{0,1:T(4,128)} fusion(f32[32,3]{0,1:T(4,128)S(1)} %copy-done.114, s32[524288]{0:T(1024)S(1)} %copy-done.119), kind=kOutput, calls=%fused_computation.126.clone.1 | convolution fusion | flops 620756992 | bytes 8388992 | tf_op jit(solution)/shard_map/while/body/eval_jaxpr/dot_general | solution.py:51
  848.0 10.5 multiply_reduce_fusion.26
  871.5 10.7 fusion.442
  882.3 10.5 fusion.445
  904.7 22.5 %fusion.444 = f32[524288,3]{0,1:T(4,128)} fusion(f32[32,3]{0,1:T(4,128)} %get-tuple-element.1353, s32[524288]{0:T(1024)S(1)} %copy-done.116), kind=kOutput, calls=%fused_computation.129.clone.1 | convolution fusion | flops 620756992 | bytes 8388992 | tf_op jit(solution)/shard_map/while/body/eval_jaxpr/dot_general | solution.py:51
  927.2 8.8 multiply_reduce_fusion.27
  947.0 21.9 %fusion.439 = f32[524288,3]{0,1:T(4,128)} fusion(f32[32,3]{0,1:T(4,128)S(1)} %copy-done.114, s32[524288]{0:T(1024)S(1)} %copy-done.119), kind=kOutput, calls=%fused_computation.126.clone.1 | convolution fusion | flops 620756992 | bytes 8388992 | tf_op jit(solution)/shard_map/while/body/eval_jaxpr/dot_general | solution.py:51
  968.9 10.6 multiply_reduce_fusion.26
  992.5 10.9 fusion.442
  1003.4 10.5 fusion.445
  1044.9 290.3 %all-reduce.5.cloned.1.call-done = (f32[2,768,192]{1,2,0:T(8,128)}, f32[2,2,768,192]{2,3,1,0:T(8,128)}, f32[2,192,768]{2,1,0:T(8,128)}, f32[2,768,512]{2,1,0:T(8,128)}, f32[512,768]{1,0:T(8,128)}) async-done(((f32[2,768,192]{1,2,0:T(8,128)}, f32[2,2,768,192]{2,3,1,0:T(8,128)}, f32[2,192,768]{2,1,0:T(8,128)}, f32[2,768,512]{2,1,0:T(8,128)}, f32[512,768]{1,0:T(8,128)}), (f32[2,768,192]{1,2,0:T(8,128)}, ...) | async-done | bytes 9437200 | tf_op jit(solution)/shard_map/psum | solution.py:445
  1343.8 51.3 %reduce-scatter.18.cloned.1.call-done = f32[512,768]{1,0:T(8,128)} async-done(((f32[2048,768]{1,0:T(8,128)}), f32[512,768]{1,0:T(8,128)}) %reduce-scatter.18.cloned.1.call-update) | async-done | bytes 1572880 | tf_op jit(solution)/shard_map/reduce_scatter | solution.py:296
  1397.1 37.6 %all-reduce = (f32[3,768]{1,0:T(4,128)S(1)}, f32[32,3]{0,1:T(4,128)}) all-reduce(f32[3,768]{1,0:T(4,128)S(1)} %pad_maximum_fusion.16, f32[32,3]{0,1:T(4,128)S(1)} %copy-done.106), channel_id=1, replica_groups=mesh['dp'=8,'tensor'=4] {'dp'}, use_global_device_ids=true, to_apply=%region_40.41 | all-reduce | flops 2400 | bytes 19200 | tf_op jit(solution)/shard_map/psum | solution.py:445
  1434.8 11.5 all-reduce.2
  (631 shorter events, 260.8 us)
Async XLA Ops:
  7.2 456.9 %copy-start = (bf16[512,768]{1,0:T(8,128)(2,1)S(1)}, bf16[512,768]{1,0:T(8,128)(2,1)}, u32[]{:S(2)}) copy-start(bf16[512,768]{1,0:T(8,128)(2,1)} %param.34) | copy-start | bytes 2359300
  7.2 37.9 %all-gather.8.cloned.1.call-start = ((), (), s32[]{:S(2)}) async-start(), calls=%async_computation.7 | async-start | bytes 3932160 | tf_op jit(solution)/shard_map/all_gather | solution.py:266
  13.7 250.0 %reduce-scatter.8.cloned.1.call-start = ((), (), s32[]{:S(2)}) async-start(), calls=%async_computation.8 | async-start | bytes 7864320 | tf_op jit(solution)/shard_map/reduce_scatter | solution.py:277
  14.5 34.5 %copy-start.78 = (bf16[768,192]{0,1:T(8,128)(2,1)}, bf16[768,192]{0,1:T(8,128)(2,1)S(1)}, u32[]{:S(2)}) copy-start(bf16[768,192]{0,1:T(8,128)(2,1)S(1)} %slice_bitcast_fusion.13) | copy-start | bytes 884740
  15.5 33.6 %copy-start.74 = (bf16[768,192]{0,1:T(8,128)(2,1)}, bf16[768,192]{0,1:T(8,128)(2,1)S(1)}, u32[]{:S(2)}) copy-start(bf16[768,192]{0,1:T(8,128)(2,1)S(1)} %get-tuple-element.804) | copy-start | bytes 884740
  15.5 33.6 %copy-start.76 = (bf16[768,192]{0,1:T(8,128)(2,1)}, bf16[768,192]{0,1:T(8,128)(2,1)S(1)}, u32[]{:S(2)}) copy-start(bf16[768,192]{0,1:T(8,128)(2,1)S(1)} %get-tuple-element.805) | copy-start | bytes 884740
  205.1 58.6 %copy-start.17 = (bf16[512,768]{1,0:T(8,128)(2,1)S(1)}, bf16[512,768]{1,0:T(8,128)(2,1)}, u32[]{:S(2)}) copy-start(bf16[512,768]{1,0:T(8,128)(2,1)} %param.25) | copy-start | bytes 2359300
  205.1 60.3 %copy-start.83 = (f32[768]{0:T(1024)S(1)}, f32[768]{0:T(1024)}, u32[]{:S(2)}) copy-start(f32[768]{0:T(1024)} %get-tuple-element.616) | copy-start | bytes 9220
  205.1 79.9 %all-gather.10.cloned.1.call-start = ((), (), s32[]{:S(2)}) async-start(), calls=%async_computation.9 | async-start | bytes 1966080 | tf_op jit(solution)/shard_map/all_gather | solution.py:344
  205.9 60.7 %copy-start.108 = (s32[2,12]{1,0:T(2,128)S(1)}, s32[2,12]{1,0:T(2,128)}, u32[]{:S(2)}) copy-start(s32[2,12]{1,0:T(2,128)} %param.36) | copy-start | bytes 292
  205.9 79.1 %copy-start.57 = (bf16[768,192]{0,1:T(8,128)(2,1)S(1)}, bf16[768,192]{0,1:T(8,128)(2,1)}, u32[]{:S(2)}) copy-start(bf16[768,192]{0,1:T(8,128)(2,1)} %get-tuple-element.803) | copy-start | bytes 884740
  205.9 109.7 %all-gather.12.cloned.1.call-start = ((), (), s32[]{:S(2)}) async-start(), calls=%async_computation.10 | async-start | bytes 3932160 | tf_op jit(solution)/shard_map/all_gather | solution.py:266
  265.4 22.0 %copy-start.94 = (f32[512]{0:T(512)}, f32[512]{0:T(512)S(1)}, u32[]{:S(2)}) copy-start(f32[512]{0:T(512)S(1)} %get-tuple-element.724) | copy-start | bytes 6148
  266.5 134.8 %reduce-scatter.10.cloned.1.call-start = ((), (), s32[]{:S(2)}) async-start(), calls=%async_computation.11 | async-start | bytes 7864320 | tf_op jit(solution)/shard_map/reduce_scatter | solution.py:277
  342.8 61.4 %copy-start.82 = (f32[768]{0:T(1024)S(1)}, f32[768]{0:T(1024)}, u32[]{:S(2)}) copy-start(f32[768]{0:T(1024)} %get-tuple-element.614) | copy-start | bytes 9220
  342.8 91.1 %all-gather.14.cloned.1.call-start = ((), (), s32[]{:S(2)}) async-start(), calls=%async_computation.12 | async-start | bytes 3932160 | tf_op jit(solution)/shard_map/all_gather | solution.py:266
  405.2 58.8 %all-gather.16.cloned.1.call-start = ((), (), s32[]{:S(2)}) async-start(), calls=%async_computation.14 | async-start | bytes 3932160 | tf_op jit(solution)/shard_map/all_gather | solution.py:286
  406.0 132.7 %reduce-scatter.14.cloned.1.call-start = ((), (), s32[]{:S(2)}) async-start(), calls=%async_computation.15 | async-start | bytes 7864320 | tf_op jit(solution)/shard_map/reduce_scatter | solution.py:296
  480.1 93.4 %all-gather.18.cloned.1.call-start = ((), (), s32[]{:S(2)}) async-start(), calls=%async_computation.16 | async-start | bytes 3932160 | tf_op jit(solution)/shard_map/all_gather | solution.py:286
  544.8 126.5 %reduce-scatter.16.cloned.1.call-start = ((), (), s32[]{:S(2)}) async-start(), calls=%async_computation.17 | async-start | bytes 7864320 | tf_op jit(solution)/shard_map/reduce_scatter | solution.py:296
  612.8 119.5 %reduce-scatter.12.cloned.1.call-start = ((), (), s32[]{:S(2)}) async-start(), calls=%async_computation.13 | async-start | bytes 7864320 | tf_op jit(solution)/shard_map/reduce_scatter | solution.py:277
  619.4 51.9 %copy-start.84 = (f32[768]{0:T(1024)S(1)}, f32[768]{0:T(1024)}, u32[]{:S(2)}) copy-start(f32[768]{0:T(1024)} %get-tuple-element.616) | copy-start | bytes 9220
  619.4 51.9 %copy-start.93 = (f32[512]{0:T(512)S(1)}, f32[512]{0:T(512)}, u32[]{:S(2)}) copy-start(f32[512]{0:T(512)} %copy-done.92) | copy-start | bytes 6148
  619.5 54.3 %copy-start.95 = (f32[512]{0:T(512)S(1)}, f32[512]{0:T(512)}, u32[]{:S(2)}) copy-start(f32[512]{0:T(512)} %copy-done.94) | copy-start | bytes 6148
  619.5 112.8 %copy-start.28 = (bf16[512,768]{1,0:T(8,128)(2,1)S(1)}, bf16[512,768]{1,0:T(8,128)(2,1)}, u32[]{:S(2)}) copy-start(bf16[512,768]{1,0:T(8,128)(2,1)} %param.27) | copy-start | bytes 2359300
  619.5 112.8 %copy-start.89 = (f32[512]{0:T(512)S(1)}, f32[512]{0:T(512)}, u32[]{:S(2)}) copy-start(f32[512]{0:T(512)} %copy-done.87) | copy-start | bytes 6148
  619.5 112.8 %copy-start.97 = (f32[512]{0:T(512)S(1)}, f32[512]{0:T(512)}, u32[]{:S(2)}) copy-start(f32[512]{0:T(512)} %copy-done.96) | copy-start | bytes 6148
  619.5 146.9 %all-gather.20.cloned.1.call-start = ((), (), s32[]{:S(2)}) async-start(), calls=%async_computation.18 | async-start | bytes 3932160 | tf_op jit(solution)/shard_map/all_gather | solution.py:286
  737.7 597.5 %all-reduce.5.cloned.1.call-start = ((), (), s32[]{:S(2)}) async-start(), calls=%async_computation.21 | async-start | bytes 18874368 | tf_op jit(solution)/shard_map/psum | solution.py:445
  777.9 28.2 %copy-start.5 = (bf16[1,512,192]{1,2,0:T(8,128)(2,1)}, bf16[1,512,192]{1,2,0:T(8,128)(2,1)S(1)}, u32[]{:S(2)}) copy-start(bf16[1,512,192]{1,2,0:T(8,128)(2,1)S(1)} %get-tuple-element.1191) | copy-start | bytes 589828 | tf_op jit(solution)/shard_map/while
  780.4 25.7 %copy-start.2 = (f32[3,512,1024]{2,1,0:T(8,128)}, f32[3,512,1024]{2,1,0:T(8,128)S(1)}, u32[]{:S(2)}) copy-start(f32[3,512,1024]{2,1,0:T(8,128)S(1)} %fusion.443) | copy-start | bytes 18874372 | tf_op jit(solution)/shard_map/while
  826.1 21.9 %copy-start.4 = (bf16[1,512,192]{1,2,0:T(8,128)(2,1)S(1)}, bf16[1,512,192]{1,2,0:T(8,128)(2,1)}, u32[]{:S(2)}) copy-start(bf16[1,512,192]{1,2,0:T(8,128)(2,1)} %get-tuple-element.1181) | copy-start | bytes 589828 | tf_op jit(solution)/shard_map/while
  882.2 11.1 copy-start.22
  882.2 11.1 copy-start.56
  899.1 28.2 %copy-start.5 = (bf16[1,512,192]{1,2,0:T(8,128)(2,1)}, bf16[1,512,192]{1,2,0:T(8,128)(2,1)S(1)}, u32[]{:S(2)}) copy-start(bf16[1,512,192]{1,2,0:T(8,128)(2,1)S(1)} %get-tuple-element.1191) | copy-start | bytes 589828 | tf_op jit(solution)/shard_map/while
  901.5 25.7 %copy-start.2 = (f32[3,512,1024]{2,1,0:T(8,128)}, f32[3,512,1024]{2,1,0:T(8,128)S(1)}, u32[]{:S(2)}) copy-start(f32[3,512,1024]{2,1,0:T(8,128)S(1)} %fusion.443) | copy-start | bytes 18874372 | tf_op jit(solution)/shard_map/while
  947.0 21.9 %copy-start.4 = (bf16[1,512,192]{1,2,0:T(8,128)(2,1)S(1)}, bf16[1,512,192]{1,2,0:T(8,128)(2,1)}, u32[]{:S(2)}) copy-start(bf16[1,512,192]{1,2,0:T(8,128)(2,1)} %get-tuple-element.1181) | copy-start | bytes 589828 | tf_op jit(solution)/shard_map/while
  992.4 10.9 copy-start.3
  1003.4 11.1 copy-start.22
  1003.4 11.1 copy-start.56
  1034.1 361.0 %reduce-scatter.18.cloned.1.call-start = ((), (), s32[]{:S(2)}) async-start(), calls=%async_computation.19 | async-start | bytes 7864320 | tf_op jit(solution)/shard_map/reduce_scatter | solution.py:296
  1039.8 410.7 %reduce-scatter.20.cloned.1.call-start = ((), (), s32[]{:S(2)}) async-start(), calls=%async_computation.20 | async-start | bytes 3932160 | tf_op jit(solution)/shard_map/reduce_scatter | solution.py:398
  1339.0 56.1 %copy-start.18 = (bf16[512,768]{1,0:T(8,128)(2,1)S(1)}, bf16[512,768]{1,0:T(8,128)(2,1)}, u32[]{:S(2)}) copy-start(bf16[512,768]{1,0:T(8,128)(2,1)} %param.25) | copy-start | bytes 2359300
  1339.0 56.1 %copy-start.86 = (f32[768]{0:T(1024)S(1)}, f32[768]{0:T(1024)}, u32[]{:S(2)}) copy-start(f32[768]{0:T(1024)} %copy-done.85) | copy-start | bytes 9220
  1339.0 56.0 %copy-start.91 = (f32[512]{0:T(512)S(1)}, f32[512]{0:T(512)}, u32[]{:S(2)}) copy-start(f32[512]{0:T(512)} %copy-done.90) | copy-start | bytes 6148
  1339.3 57.8 %copy-start.106 = (f32[32,3]{0,1:T(4,128)S(1)}, f32[32,3]{0,1:T(4,128)}, u32[]{:S(2)}) copy-start(f32[32,3]{0,1:T(4,128)} %get-tuple-element.254) | copy-start | bytes 1156
  1339.6 106.7 %copy-start.99 = (f32[512]{0:T(512)S(1)}, f32[512]{0:T(512)}, u32[]{:S(2)}) copy-start(f32[512]{0:T(512)} %copy-done.98) | copy-start | bytes 6148
  1339.6 106.7 %copy-start.109 = (f32[11]{0:T(128)S(1)}, f32[11]{0:T(128)}, u32[]{:S(2)}) copy-start(f32[11]{0:T(128)} %constant.152) | copy-start | bytes 136
  (133 other events, 401.4 us)
Sparse Core Ops, SparseCore 0:
  13.8 31.2 all-gather.7
  205.3 58.3 reduce-scatter.7
  265.3 19.6 all-gather.9
  287.1 28.5 all-gather.11
  342.9 58.3 reduce-scatter.9
  405.4 28.5 all-gather.13
  435.5 28.5 all-gather.15
  480.3 58.3 reduce-scatter.13
  545.0 28.5 all-gather.17
  613.0 58.3 reduce-scatter.15
  673.9 58.3 reduce-scatter.11
  737.8 28.5 all-gather.19
  1034.2 300.9 all-reduce.4
  1337.7 57.2 reduce-scatter.17
  1398.6 37.9 reduce-scatter.19
where the time goes:
time: 1470 us
  waiting for transfers between devices  784 us (53%)
  matrix products  404 us (27%)
  local copies, waits for them, and re-layouts  97.5 us (7%)
  other arithmetic  79.7 us (5%)
  blocking collectives  49.1 us (3%)
  loops' own time  35.6 us (2%)
  between operations  15.1 us (1%)
    psum x1, waiting for transfers between devices, on_device(): lax.psum((query_grad, keyvalue_grad, output_grad, table_grad, inner_grad,...  290 us
    reduce_scatter x3, waiting for transfers between devices, project_out(): lax.psum_scatter(jnp.dot(part_rows, weight, preferred_element_type=jnp.fl...  175 us
    dot_general x8, matrix products, block_bias(): lax.dot_general(bias_table, onehot, (((0,), (1,)), ((), ())), precision=l...  172 us
    reduce_scatter x3, waiting for transfers between devices, scatter_grads(): lax.psum_scatter(dot_cols(part_rows, weight_cat), 'tensor', scatter_dimen...  161 us
    all_gather x3, waiting for transfers between devices, project_in(): gathered = lax.all_gather(normed, 'tensor', axis=0, tiled=True)  82.1 us
    dot_general x16, matrix products, block_scores(): jnp.einsum('qhd,khd->hqk', split_query, split_key, preferred_element_type...  63.1 us
    all_gather x3, waiting for transfers between devices, gather_grads(): return lax.all_gather(grad_rows, 'tensor', axis=0, tiled=True)  55.9 us
    dot_general x4, matrix products, attend_slot_back(): lax.dot_general(onehot, flat_grad, (((0,), (1,)), ((), ())), precision=la...  42.6 us
  transfers between devices with their start and end apart: 15, of which 14 were waited for; matrix products, arithmetic and copies ran while one was open for 5% of the time, Pallas kernels for 0%

commit v1 on v0

v1 whole, which is shorter than its diff:
```python
import math

import jax
import jax.numpy as jnp
import numpy as np
from jax import lax
from jax.experimental import pallas as pl
from jax.experimental.pallas import tpu as pltpu
from jax.sharding import PartitionSpec as P

D = 768
DH = 64
BUCKETS = 32
MAXDIST = 128
SLOT = 1024
MEM = 512
NORM_EPS = 1e-06
NEG_FILL = -1e30
BQ = 256
VM = pl.BlockSpec(memory_space=pltpu.VMEM)
SM = pl.BlockSpec(memory_space=pltpu.SMEM)
NT = (((1,), (1,)), ((), ()))
NN = (((1,), (0,)), ((), ()))
TN = (((0,), (0,)), ((), ()))
f32, bf16 = jnp.float32, jnp.bfloat16


def dg(a, b, dims):
    return lax.dot_general(a, b, dims, preferred_element_type=f32)


def blk(i):
    return pl.ds(pl.multiple_of(i * BQ, BQ), BQ)


def put_heads(ref, rows, wide):
    for h in range(3):
        ref[h, rows, :] = wide[:, h * 64:(h + 1) * 64].astype(ref.dtype)


def project(n_ref, w, out3):
    def body(i, _):
        put_heads(out3, blk(i), dg(n_ref[blk(i), :], w, NT))
        return 0
    lax.fori_loop(0, n_ref.shape[0] // BQ, body, 0)


def fill_bias(base_ref, bias_scr):
    span = base_ref.shape[1]
    for h in range(3):
        row = jnp.broadcast_to(base_ref[h:h + 1, :], (BQ, span))
        bias_scr[h] = pltpu.roll(row, 0, 1, stride=1, stride_axis=0)[:, :768]


def softmax_parts(s):
    m = jnp.max(s, axis=1, keepdims=True)
    e = jnp.exp(s - m)
    rl = 1.0 / jnp.sum(e, axis=1, keepdims=True)
    return e, m, rl


SELF_W = (256, 384, 512, 768)
CROSS_W = (128, 256, 512)


def self_scores(q, k, bias, ds, q0, width):
    s = dg(q, k, NT) + bias
    kpos = lax.broadcasted_iota(jnp.int32, (BQ, width), 1) + (q0 + BQ - width)
    return jnp.where(kpos >= ds, s, NEG_FILL)


def self_fwd_kernel(win, n_ref, w_ref, ds_ref, base_ref, q3, k3, v3, ctx_ref, st_ref, out_ref, bias_scr, c3):
    fill_bias(base_ref, bias_scr)
    project(n_ref, w_ref[0:192, :], q3)
    project(n_ref, w_ref[192:384, :], k3)
    project(n_ref, w_ref[384:576, :], v3)

    def block(i, _):
        q0 = pl.multiple_of(i * BQ, BQ)
        rows = pl.ds(q0, BQ)

        @pl.when(win[i] == 0)
        def _():
            ctx_ref[rows, :] = jnp.zeros((BQ, 192), bf16)
            st_ref[rows, :] = jnp.zeros((BQ, 8), f32)

        for n, width in enumerate(SELF_W):
            @pl.when(win[i] == n + 1)
            def _(width=width):
                keys = pl.ds(pl.multiple_of(q0 + (BQ - width), 128), width)
                ds = ds_ref[rows, :]
                for h in range(3):
                    s = self_scores(q3[h, rows, :], k3[h, keys, :], bias_scr[h, :, 768 - width:], ds, q0, width)
                    e, m, rl = softmax_parts(s)
                    p = (e * rl).astype(bf16)
                    c = dg(p, v3[h, keys, :], NN)
                    c = jnp.where(ds < 4096, c, 0.0)
                    ctx_ref[rows, h * 64:(h + 1) * 64] = c.astype(bf16)
                    st_ref[rows, h:h + 1] = m
                    st_ref[rows, h + 3:h + 4] = rl
        out_ref[rows, :] = dg(ctx_ref[rows, :], w_ref[576:768, :], NN)
        return 0
    lax.fori_loop(0, n_ref.shape[0] // BQ, block, 0)


def params(flops, byts, vmem=48):
    return dict(compiler_params=pltpu.CompilerParams(vmem_limit_bytes=vmem << 20),
                cost_estimate=pl.CostEstimate(flops=int(flops), bytes_accessed=int(byts), transcendentals=0))


def self_fwd(win, n, w, ds, base):
    R = n.shape[0]
    sd = jax.ShapeDtypeStruct
    return pl.pallas_call(
        self_fwd_kernel,
        in_specs=[SM, VM, VM, VM, VM],
        out_specs=[VM] * 6,
        out_shape=[sd((3, R, 64), bf16)] * 3 + [sd((R, 192), bf16), sd((R, 8), f32), sd((R, 768), f32)],
        scratch_shapes=[pltpu.VMEM((3, BQ, 768), f32), pltpu.VMEM((3, R, 64), f32)],
        name="self_fwd", **params(6e9, 10e6))(win, n, w, ds, base)


def diagonal_sums(scr, h):
    span = scr.shape[2]
    slabs = [scr[h, 8 * a:8 * a + 8, :] for a in range(BQ // 8)]
    step = 8
    while len(slabs) > 1:
        slabs = [slabs[j] + pltpu.roll(slabs[j + 1], span - step, 1) for j in range(0, len(slabs), 2)]
        step *= 2
    acc = slabs[0]
    row = lax.broadcasted_iota(jnp.int32, acc.shape, 0)
    for bit in (1, 2, 4):
        acc = jnp.where((row & bit) > 0, pltpu.roll(acc, span - bit, 1), acc)
    return jnp.sum(acc, axis=0, keepdims=True)


def self_bwd_kernel(win, b_ref, n_ref, w_ref, ds_ref, base_ref, q3, k3, v3, ctx_ref, st_ref,
                    dw_ref, dn_ref, db_ref, bias_scr, dbias_scr, g3, dq, dk, dv):
    R = n_ref.shape[0]
    fill_bias(base_ref, bias_scr)
    dbias_scr[...] = jnp.zeros(dbias_scr.shape, f32)
    dk[...] = jnp.zeros(dk.shape, f32)
    dv[...] = jnp.zeros(dv.shape, f32)

    def gpart(i, _):
        rows = blk(i)
        g = dg(b_ref[rows, :], w_ref[576:768, :], NT).astype(bf16)
        g = jnp.where(ds_ref[rows, :] < 4096, g, jnp.zeros_like(g))
        put_heads(g3, rows, g)
        return 0
    lax.fori_loop(0, R // BQ, gpart, 0)

    def block(i, _):
        q0 = pl.multiple_of(i * BQ, BQ)
        rows = pl.ds(q0, BQ)

        @pl.when(win[i] == 0)
        def _():
            dq[rows, :] = jnp.zeros((BQ, 192), bf16)

        for n, width in enumerate(SELF_W):
            @pl.when(win[i] == n + 1)
            def _(width=width):
                keys = pl.ds(pl.multiple_of(q0 + (BQ - width), 128), width)
                ds = ds_ref[rows, :]
                for h in range(3):
                    q = q3[h, rows, :]
                    k = k3[h, keys, :]
                    g = g3[h, rows, :]
                    s = self_scores(q, k, bias_scr[h, :, 768 - width:], ds, q0, width)
                    p = jnp.exp(s - st_ref[rows, h:h + 1]) * st_ref[rows, h + 3:h + 4]
                    wg = dg(g, v3[h, keys, :], NT)
                    inner = jnp.sum(p * wg, axis=1, keepdims=True)
                    sg = (p * (wg - inner)).astype(bf16)
                    dv[h, keys, :] += dg(p.astype(bf16), g, TN)
                    dk[h, keys, :] += dg(sg, q, TN)
                    dq[rows, h * 64:(h + 1) * 64] = dg(sg, k, NN).astype(bf16)
                    dbias_scr[h, :, 768 - width:768] += sg.astype(f32)
        return 0
    lax.fori_loop(0, R // BQ, block, 0)
    finish_bwd(dq, dk, dv, n_ref, n_ref, b_ref, ctx_ref, w_ref, dw_ref)

    def back(i, _):
        rows = blk(i)
        dkb = jnp.concatenate([dk[h, rows, :] for h in range(3)], axis=1).astype(bf16)
        dvb = jnp.concatenate([dv[h, rows, :] for h in range(3)], axis=1).astype(bf16)
        dn_ref[rows, :] = (dg(dq[rows, :], w_ref[0:192, :], NN) + dg(dkb, w_ref[192:384, :], NN)
                           + dg(dvb, w_ref[384:576, :], NN))
        return 0
    lax.fori_loop(0, R // BQ, back, 0)
    for h in range(3):
        db_ref[h:h + 1, :] = diagonal_sums(dbias_scr, h)


def finish_bwd(dq, dk, dv, nq_ref, nk_ref, b_ref, ctx_ref, w_ref, dw_ref):
    dw_ref[0:192, :] = dg(dq[...], nq_ref[...], TN).astype(dw_ref.dtype)
    for slot, src in ((1, dk), (2, dv)):
        wide = jnp.concatenate([src[h] for h in range(3)], axis=1).astype(bf16)
        dw_ref[192 * slot:192 * slot + 192, :] = dg(wide, nk_ref[...], TN).astype(dw_ref.dtype)
    dw_ref[576:768, :] = dg(ctx_ref[...], b_ref[...], TN).astype(dw_ref.dtype)


def self_bwd(win, b, n, w, ds, base, q3, k3, v3, ctx, st):
    R = n.shape[0]
    sd = jax.ShapeDtypeStruct
    return pl.pallas_call(
        self_bwd_kernel,
        in_specs=[SM] + [VM] * 10,
        out_specs=[VM] * 3,
        out_shape=[sd((768, 768), bf16), sd((R, 768), f32), sd((3, 1024), f32)],
        scratch_shapes=[pltpu.VMEM((3, BQ, 768), f32), pltpu.VMEM((3, BQ, 1024), f32), pltpu.VMEM((3, R, 64), bf16),
                        pltpu.VMEM((R, 192), bf16), pltpu.VMEM((3, R, 64), f32), pltpu.VMEM((3, R, 64), f32)],
        name="self_bwd", **params(14e9, 12e6))(win, b, n, w, ds, base, q3, k3, v3, ctx, st)


def cross_scores(q, k, tseg, sseg):
    return jnp.where(tseg == sseg, dg(q, k, NT), NEG_FILL)


def cross_kv_kernel(m_ref, w_ref, k3, v3):
    project(m_ref, w_ref[192:384, :], k3)
    project(m_ref, w_ref[384:576, :], v3)


def cross_kv(mem, w):
    sd = jax.ShapeDtypeStruct
    M = mem.shape[0]
    return pl.pallas_call(cross_kv_kernel, in_specs=[VM, VM], out_specs=[VM, VM],
                          out_shape=[sd((3, M, 64), bf16)] * 2, name="cross_kv", **params(1.5e9, 3e6, 32))(mem, w)


def cross_fwd_kernel(win, n_ref, w_ref, tseg_ref, sseg_ref, k3, v3, q3, ctx_ref, st_ref, out_ref):
    project(n_ref, w_ref[0:192, :], q3)

    def block(i, _):
        rows = blk(i)

        @pl.when(win[0, i] == 0)
        def _():
            ctx_ref[rows, :] = jnp.zeros((BQ, 192), bf16)
            st_ref[rows, :] = jnp.zeros((BQ, 8), f32)

        for n, width in enumerate(CROSS_W):
            @pl.when(win[0, i] == n + 1)
            def _(width=width):
                keys = pl.ds(pl.multiple_of(win[1, i], 128), width)
                tseg = tseg_ref[rows, :]
                sseg = sseg_ref[:, keys]
                for h in range(3):
                    s = cross_scores(q3[h, rows, :], k3[h, keys, :], tseg, sseg)
                    e, m, rl = softmax_parts(s)
                    c = dg((e * rl).astype(bf16), v3[h, keys, :], NN)
                    c = jnp.where(tseg > 0, c, 0.0)
                    ctx_ref[rows, h * 64:(h + 1) * 64] = c.astype(bf16)
                    st_ref[rows, h:h + 1] = m
                    st_ref[rows, h + 3:h + 4] = rl
        out_ref[rows, :] = dg(ctx_ref[rows, :], w_ref[576:768, :], NN)
        return 0
    lax.fori_loop(0, n_ref.shape[0] // BQ, block, 0)


def cross_fwd(win, n, w, tseg, sseg, k3, v3):
    R = n.shape[0]
    sd = jax.ShapeDtypeStruct
    return pl.pallas_call(
        cross_fwd_kernel,
        in_specs=[SM] + [VM] * 6, out_specs=[VM] * 4,
        out_shape=[sd((3, R, 64), bf16), sd((R, 192), bf16), sd((R, 8), f32), sd((R, 768), f32)],
        name="cross_fwd", **params(3e9, 8e6, 32))(win, n, w, tseg, sseg, k3, v3)


def cross_bwd_kernel(win, b_ref, n_ref, m_ref, w_ref, tseg_ref, sseg_ref, q3, k3, v3, ctx_ref, st_ref,
                     dw_ref, dn_ref, dm_ref, g3, dq, dk, dv):
    R = n_ref.shape[0]
    dk[...] = jnp.zeros(dk.shape, f32)
    dv[...] = jnp.zeros(dv.shape, f32)

    def block(i, _):
        rows = blk(i)
        tseg = tseg_ref[rows, :]
        g = dg(b_ref[rows, :], w_ref[576:768, :], NT).astype(bf16)
        g = jnp.where(tseg > 0, g, jnp.zeros_like(g))
        put_heads(g3, pl.ds(0, BQ), g)

        @pl.when(win[0, i] == 0)
        def _():
            dq[rows, :] = jnp.zeros((BQ, 192), bf16)

        for n, width in enumerate(CROSS_W):
            @pl.when(win[0, i] == n + 1)
            def _(width=width):
                keys = pl.ds(pl.multiple_of(win[1, i], 128), width)
                sseg = sseg_ref[:, keys]
                for h in range(3):
                    q = q3[h, rows, :]
                    k = k3[h, keys, :]
                    gh = g3[h]
                    s = cross_scores(q, k, tseg, sseg)
                    p = jnp.exp(s - st_ref[rows, h:h + 1]) * st_ref[rows, h + 3:h + 4]
                    wg = dg(gh, v3[h, keys, :], NT)
                    inner = jnp.sum(p * wg, axis=1, keepdims=True)
                    sg = (p * (wg - inner)).astype(bf16)
                    dv[h, keys, :] += dg(p.astype(bf16), gh, TN)
                    dk[h, keys, :] += dg(sg, q, TN)
                    dq[rows, h * 64:(h + 1) * 64] = dg(sg, k, NN).astype(bf16)
        dn_ref[rows, :] = dg(dq[rows, :], w_ref[0:192, :], NN)
        return 0
    lax.fori_loop(0, R // BQ, block, 0)
    finish_bwd(dq, dk, dv, n_ref, m_ref, b_ref, ctx_ref, w_ref, dw_ref)

    def back(i, _):
        rows = blk(i)
        dkb = jnp.concatenate([dk[h, rows, :] for h in range(3)], axis=1).astype(bf16)
        dvb = jnp.concatenate([dv[h, rows, :] for h in range(3)], axis=1).astype(bf16)
        dm_ref[rows, :] = dg(dkb, w_ref[192:384, :], NN) + dg(dvb, w_ref[384:576, :], NN)
        return 0
    lax.fori_loop(0, m_ref.shape[0] // BQ, back, 0)


def cross_bwd(win, b, n, mem, w, tseg, sseg, q3, k3, v3, ctx, st):
    R, M = n.shape[0], mem.shape[0]
    sd = jax.ShapeDtypeStruct
    return pl.pallas_call(
        cross_bwd_kernel,
        in_specs=[SM] + [VM] * 11, out_specs=[VM] * 3,
        out_shape=[sd((768, 768), bf16), sd((R, 768), f32), sd((M, 768), f32)],
        scratch_shapes=[pltpu.VMEM((3, BQ, 64), bf16), pltpu.VMEM((R, 192), bf16), pltpu.VMEM((3, M, 64), f32),
                        pltpu.VMEM((3, M, 64), f32)],
        name="cross_bwd", **params(8e9, 12e6, 40))(win, b, n, mem, w, tseg, sseg, q3, k3, v3, ctx, st)


def bucket_of(spread):
    exact_count = BUCKETS // 2
    if spread < exact_count:
        return spread
    larger = exact_count + math.floor(
        math.log(spread / exact_count) / math.log(MAXDIST / exact_count) * (BUCKETS - exact_count)
    )
    return min(larger, BUCKETS - 1)


def bias_lanes():
    lane = np.arange(1024)
    distance = 512 - np.where(lane < 768, lane, lane - 1024)
    buckets = np.array([bucket_of(max(int(n), 0)) for n in distance], np.int32)
    return distance, buckets


def base_rows(table):
    distance, buckets = bias_lanes()
    onehot = (jnp.asarray(buckets)[None, :] == jnp.arange(BUCKETS)[:, None]).astype(f32)
    rows = lax.dot_general(table, onehot, TN, precision=lax.Precision.HIGHEST, preferred_element_type=f32)
    return jnp.where(jnp.asarray(distance >= 0)[None, :], rows, NEG_FILL)


def bucket_sums(lane_sums):
    distance, buckets = bias_lanes()
    onehot = (jnp.asarray(buckets)[:, None] == jnp.arange(BUCKETS)[None, :]) & jnp.asarray(distance >= 0)[:, None]
    return lax.dot_general(
        onehot.astype(f32), lane_sums, (((0,), (1,)), ((), ())), precision=lax.Precision.HIGHEST,
        preferred_element_type=f32)


def running_sum(lengths):
    tri = np.tril(np.ones((lengths.shape[0],) * 2, bool))
    return jnp.sum(jnp.where(tri, lengths[None, :], 0), axis=1)


def slot_layout(tl, sl):
    ends = running_sum(tl)
    starts = ends - tl
    total = jnp.sum(tl)
    pos = jnp.arange(SLOT, dtype=jnp.int32)
    past = pos[:, None] >= ends[None, :]
    live = pos < total
    tseg = jnp.where(live, jnp.sum(past.astype(jnp.int32), axis=1) + 1, -1)
    doc_start = jnp.where(live, jnp.max(jnp.where(past, ends[None, :], 0), axis=1), 1 << 20)
    sends = running_sum(sl)
    spos = jnp.arange(MEM, dtype=jnp.int32)
    sseg = jnp.where(spos < jnp.sum(sl), jnp.sum((spos[:, None] >= sends[None, :]).astype(jnp.int32), axis=1) + 1, 0)
    q0 = jnp.arange(0, SLOT, BQ, dtype=jnp.int32)
    alive = q0 < total
    first = jnp.max(jnp.where(q0[:, None] >= ends[None, :], ends[None, :], 0), axis=1)
    need = q0 + BQ - (first // 128) * 128
    swin = 1 + sum((need > width).astype(jnp.int32) for width in SELF_W[:-1])
    swin = jnp.where(alive, swin, 0)
    last = jnp.minimum(q0 + BQ - 1, total - 1)
    low = jnp.sum(jnp.where(ends[None, :] <= q0[:, None], sl[None, :], 0), axis=1)
    high = jnp.sum(jnp.where(starts[None, :] <= last[:, None], sl[None, :], 0), axis=1)
    at1 = (low // 128) * 128
    at2 = jnp.minimum(at1, MEM - 256)
    fits1 = high - at1 <= 128
    fits2 = high - at2 <= 256
    cwin = jnp.where(fits1, 1, jnp.where(fits2, 2, 3))
    cat = jnp.where(fits1, at1, jnp.where(fits2, at2, 0))
    cross_win = jnp.stack((jnp.where(alive, cwin, 0), jnp.where(alive, cat, 0)))
    return tseg[:, None], doc_start[:, None], sseg[None, :], swin, cross_win


def rms_normed(rows_in, gain_row):
    inverse_rms = lax.rsqrt(jnp.mean(rows_in * rows_in, axis=-1, keepdims=True) + NORM_EPS)
    return (rows_in * inverse_rms * gain_row[None, :]).astype(bf16)


def rms_back(rows_in, gain_row, grad):
    r = lax.rsqrt(jnp.mean(rows_in * rows_in, axis=-1, keepdims=True) + NORM_EPS)
    scaled = grad * gain_row[None, :]
    back = r * scaled - rows_in * (r * r * r) * jnp.mean(scaled * rows_in, axis=-1, keepdims=True)
    return back, jnp.sum(grad * rows_in * r, axis=0)


def gated_unit(gate_in, up_in):
    return jax.nn.gelu(gate_in, approximate=True) * up_in


CORE = [(i, i ^ 1) for i in range(4)]
CHIP = [(i, i ^ 2) for i in range(4)]


def swap_core(v):
    return lax.ppermute(v, "tensor", CORE)


def swap_chip(v):
    return lax.ppermute(v, "tensor", CHIP)


def swap_dp(v, bit):
    return lax.ppermute(v, "dp", [(i, i ^ (1 << bit)) for i in range(lax.axis_size("dp"))])


def dp_bits():
    return int(math.log2(lax.axis_size("dp")))


def add16(a, b):
    return (a.astype(f32) + b.astype(f32)).astype(bf16)


def reduce_grads(own, away):
    d = lax.axis_index("dp")
    total = add16(own, swap_chip(away))
    for bit in range(dp_bits()):
        mine = lax.shift_right_logical(d, bit) & 1
        halves = total.reshape((2, total.shape[0] // 2) + total.shape[1:])
        sent = swap_dp(lax.dynamic_index_in_dim(halves, 1 - mine, 0, False), bit)
        total = add16(lax.dynamic_index_in_dim(halves, mine, 0, False), sent)
    for bit in reversed(range(dp_bits())):
        mine = lax.shift_right_logical(d, bit) & 1
        other = swap_dp(total, bit)
        total = jnp.where(mine == 0, jnp.concatenate((total, other)), jnp.concatenate((other, total)))
    return total.astype(f32)


def sum_small(v, core):
    if core:
        v = v + swap_core(v)
    v = v + swap_chip(v)
    for bit in range(dp_bits()):
        v = v + swap_dp(v, bit)
    return v


def after(value, *earlier):
    return lax.optimization_barrier((value,) + earlier)[0]


def on_device(tokens, memory, cotangent, norm_gains, query_weight, keyvalue_weight, output_weight, bias_table,
              inner_weight, outer_weight, target_lengths, source_lengths):
    t = lax.axis_index("tensor")
    core = t & 1
    slot = lax.shift_right_logical(t, 1)
    tl = lax.dynamic_index_in_dim(target_lengths, slot, 0, False)
    sl = lax.dynamic_index_in_dim(source_lengths, slot, 0, False)
    tseg, doc_start, sseg, swin, cwin = slot_layout(tl, sl)

    def joined(rows):
        other = swap_core(rows)
        return jnp.where(core == 0, jnp.concatenate((rows, other)), jnp.concatenate((other, rows)))

    def mine_of(rows):
        half = rows.shape[0] // 2
        return lax.dynamic_slice_in_dim(rows, core * half, half, 0)

    def theirs_of(rows):
        half = rows.shape[0] // 2
        return lax.dynamic_slice_in_dim(rows, (1 - core) * half, half, 0)

    def scattered(rows):
        return mine_of(rows) + swap_core(theirs_of(rows))

    stacks = [
        jnp.concatenate((query_weight[i].T, keyvalue_weight[i, 0].T, keyvalue_weight[i, 1].T, output_weight[i]))
        for i in range(2)
    ]
    away_self = swap_chip(stacks[0])
    away_table = swap_chip(bias_table)
    away_cross = swap_chip(after(stacks[1], away_self))
    away_inner = swap_chip(after(inner_weight, away_cross))
    away_outer = swap_chip(after(outer_weight, away_inner))
    wself = (stacks[0], away_self)
    wcross = (stacks[1], away_cross)
    winner = (inner_weight, away_inner)
    wouter = (outer_weight, away_outer)
    bases = (base_rows(bias_table), base_rows(away_table))

    residual = joined(tokens).astype(f32)
    mem = joined(memory)
    cot = joined(cotangent)
    n1 = rms_normed(residual, norm_gains[0])
    fs = [self_fwd(swin, n1, wself[p], doc_start, bases[p]) for p in range(2)]
    part = fs[0][5] + fs[1][5]
    after_self = residual + (part + swap_core(part))
    kv = [cross_kv(mem, wcross[p]) for p in range(2)]
    n2 = rms_normed(after_self, norm_gains[1])
    fc = [cross_fwd(cwin, n2, wcross[p], tseg, sseg, *kv[p]) for p in range(2)]
    part = fc[0][3] + fc[1][3]
    after_cross = after_self + (part + swap_core(part))
    n3 = rms_normed(after_cross, norm_gains[2])

    outs, thirds, keep = [], [], []
    for p in range(2):
        wi, wo = winner[p], wouter[p]
        gate = dg(n3, wi[0], NN)
        up = dg(n3, wi[1], NN)
        hidden, pull = jax.vjp(gated_unit, gate, up)
        hidden = hidden.astype(bf16)
        gate_grad, up_grad = pull(dg(cot, wo, NT))
        gate_grad, up_grad = gate_grad.astype(bf16), up_grad.astype(bf16)
        outs.append(dg(hidden, wo, NN))
        thirds.append(dg(gate_grad, wi[0], NT) + dg(up_grad, wi[1], NT))
        keep.append((hidden, gate_grad, up_grad))
    part = thirds[0] + thirds[1]
    third_grad = part + swap_core(part)
    output_rows = (mine_of(after_cross) + scattered(outs[0] + outs[1])).astype(bf16)
    dinner = [jnp.concatenate((dg(n3, keep[p][1], TN), dg(n3, keep[p][2], TN))).astype(bf16) for p in range(2)]
    douter = [dg(keep[p][0], cot, TN).astype(bf16) for p in range(2)]
    inner_sum = reduce_grads(*dinner).reshape(inner_weight.shape)
    outer_sum = reduce_grads(*douter)

    back, gain2 = rms_back(after_cross, norm_gains[2], third_grad)
    cross_out_grad = cot.astype(f32) + back
    branch = cross_out_grad.astype(bf16)
    bc = [None, None]
    for p in (1, 0):
        bc[p] = cross_bwd(cwin, branch, n2, mem, wcross[p], tseg, sseg, fc[p][0], *kv[p], *fc[p][1:3])
    part = bc[0][1] + bc[1][1]
    second_grad = part + swap_core(part)
    memory_grad = scattered(bc[0][2] + bc[1][2])
    cross_sum = reduce_grads(bc[0][0], bc[1][0])

    back, gain1 = rms_back(after_self, norm_gains[1], second_grad)
    self_out_grad = cross_out_grad + back
    branch = self_out_grad.astype(bf16)
    bs = [None, None]
    for p in (1, 0):
        bs[p] = self_bwd(swin, branch, n1, wself[p], doc_start, bases[p], *fs[p][:5])
    self_sum = reduce_grads(bs[0][0], bs[1][0])
    first_grad = scattered(bs[0][1] + bs[1][1])
    back, gain0 = rms_back(tokens.astype(f32), norm_gains[0], first_grad)
    tokens_grad = mine_of(self_out_grad) + back
    lanes = bs[0][2] + swap_chip(bs[1][2])
    for bit in range(dp_bits()):
        lanes = lanes + swap_dp(lanes, bit)
    table_sum = bucket_sums(lanes)
    gain0 = gain0 + swap_core(gain0)
    gains_total = sum_small(jnp.stack((gain0, gain1, gain2)), False)

    sq_self = (self_sum * self_sum).reshape(4, -1, D)
    sq_cross = (cross_sum * cross_sum).reshape(4, -1, D)
    sq_inner = inner_sum * inner_sum
    sq_outer = outer_sum * outer_sum
    ms, mc = jnp.sum(sq_self, axis=1), jnp.sum(sq_cross, axis=1)
    model_part = jnp.concatenate(
        (ms[:1], mc[:1], ms[1:3], mc[1:3], jnp.sum(sq_inner, axis=2), ms[3:], mc[3:], jnp.sum(sq_outer, axis=0)[None]))
    model_total = model_part + swap_core(model_part)
    model_total = model_total + swap_chip(model_total)
    hidden_units = outer_weight.shape[0] * lax.axis_size("tensor")
    divisors = jnp.array([D] * 6 + [hidden_units] * 2 + [D] * 2 + [hidden_units], f32)
    model_stats = model_total / divisors[:, None]
    hs, hc = jnp.sum(sq_self, axis=2) / D, jnp.sum(sq_cross, axis=2) / D
    head_stats = jnp.concatenate((hs[:1], hc[:1], hs[1:3], hc[1:3]))
    projection_stats = jnp.stack((hs[3], hc[3]))
    unit_stats = jnp.concatenate((jnp.sum(sq_inner, axis=1), jnp.sum(sq_outer, axis=1)[None])) / D
    sw = self_sum.reshape(4, -1, D)
    cw = cross_sum.reshape(4, -1, D)
    query_grad = jnp.stack((sw[0].T, cw[0].T))
    keyvalue_grad = jnp.stack((jnp.stack((sw[1].T, sw[2].T)), jnp.stack((cw[1].T, cw[2].T))))
    output_grad = jnp.stack((sw[3], cw[3]))
    return (output_rows, tokens_grad, memory_grad, gains_total, query_grad, keyvalue_grad, output_grad, table_sum,
            inner_sum, outer_sum, model_stats, head_stats, projection_stats, unit_stats)


def solution(mesh):
    rows = P(("dp", "tensor"), None)
    in_specs = (rows, rows, rows, P(), P(None, None, "tensor"), P(None, None, None, "tensor"), P(None, "tensor", None),
                P(None, "tensor"), P(None, None, "tensor"), P("tensor", None), P("dp", None), P("dp", None))
    out_specs = (rows, rows, rows, P(), P(None, None, "tensor"), P(None, None, None, "tensor"),
                 P(None, "tensor", None), P(None, "tensor"), P(None, None, "tensor"), P("tensor", None), P(),
                 P(None, "tensor"), P(None, "tensor"), P(None, "tensor"))
    return jax.shard_map(on_device, mesh=mesh, in_specs=in_specs, out_specs=out_specs, check_vma=False)
```

time: 1470 us -> 510 us (0.35)
  waiting for transfers between devices: 784 us -> 198 us
  matrix products: 404 us -> 38.5 us
  Pallas kernels: 0 us -> 93.2 us
  local copies, waits for them, and re-layouts: 97.5 us -> 32.3 us
  starting transfers between devices: 1.41 us -> 59.5 us
  blocking collectives: 49.1 us -> 0 us
  loops' own time: 35.6 us -> 0 us
    dot_general x89 -> x21, matrix products: 404 us -> 38.5 us  [the longest x18 37.1 us: dg(): return lax.dot_general(a, b, dims, preferred_element_type=f32)]
    reduce_scatter x7 -> x0, waiting for transfers between devices: 336 us -> none  [the longest x3 175 us: project_out(): lax.psum_scatter(jnp.dot(part_rows, weight, preferred_element_type=jnp.fl...]
    psum x1 -> x0, waiting for transfers between devices: 290 us -> none  [on_device(): lax.psum((query_grad, keyvalue_grad, output_grad, table_grad, inner_grad,...]
    ppermute x0 -> x54, waiting for transfers between devices: none -> 198 us  [the longest x12 104 us: swap_chip(): return lax.ppermute(v, 'tensor', CHIP)]
    all_gather x7 -> x0, waiting for transfers between devices: 156 us -> none  [the longest x3 82.1 us: project_in(): gathered = lax.all_gather(normed, 'tensor', axis=0, tiled=True)]
    pallas_call x0 -> x10, Pallas kernels: none -> 93.2 us  [the longest x2 33.4 us: self_bwd(): pl.pallas_call(self_bwd_kernel, in_specs=[SM] + [VM] * 10, out_specs=[VM]...]
    ppermute x0 -> x54, starting transfers between devices: none -> 59.5 us  [the longest x30 49.2 us: swap_dp(): lax.ppermute(v, 'dp', [(i, i ^ 1 << bit) for i in range(lax.axis_size('dp...]
    psum x2 -> x0, blocking collectives: 49.1 us -> none  [the longest x1 37.6 us: on_device(): lax.psum((query_grad, keyvalue_grad, output_grad, table_grad, inner_grad,...]
  transfers between devices with their start and end apart: 15 -> 54, of which waited for: 14 -> 28; matrix products, arithmetic and copies ran while one was open for 5% -> 20% of each run, Pallas kernels for 0% -> 13%
where the time goes in v1:
time: 510 us; the launch traced here: 505 us
  waiting for transfers between devices  198 us (39%)
  Pallas kernels  93.2 us (18%)
  other arithmetic  80 us (16%)
  starting transfers between devices  59.5 us (12%)
  matrix products  38.5 us (8%)
  local copies, waits for them, and re-layouts  32.3 us (6%)
    ppermute x12, waiting for transfers between devices, swap_chip(): return lax.ppermute(v, 'tensor', CHIP)  104 us
    ppermute x30, waiting for transfers between devices, swap_dp(): lax.ppermute(v, 'dp', [(i, i ^ 1 << bit) for i in range(lax.axis_size('dp...  91.4 us
    ppermute x30, starting transfers between devices, swap_dp(): lax.ppermute(v, 'dp', [(i, i ^ 1 << bit) for i in range(lax.axis_size('dp...  49.2 us
    dot_general x18, matrix products, dg(): return lax.dot_general(a, b, dims, preferred_element_type=f32)  37.1 us
    pallas_call x2, Pallas kernels, self_bwd(): pl.pallas_call(self_bwd_kernel, in_specs=[SM] + [VM] * 10, out_specs=[VM]...  33.4 us
    pallas_call x2, Pallas kernels, self_fwd(): pl.pallas_call(self_fwd_kernel, in_specs=[SM, VM, VM, VM, VM], out_specs=...  26.4 us
    pallas_call x2, Pallas kernels, cross_bwd(): pl.pallas_call(cross_bwd_kernel, in_specs=[SM] + [VM] * 11, out_specs=[VM...  18.1 us
    unnamed x226, local copies, waits for them, and re-layouts  12 us
  transfers between devices with their start and end apart: 54, of which 28 were waited for; matrix products, arithmetic and copies ran while one was open for 20% of the time, Pallas kernels for 13%

profile of v1, /device:TPU:0, one launch (start us, length us, event | category | flops | bytes accessed | tf_op | source)
XLA Modules:
  0.0 505.5 jit_solution(15071534804739420259)
XLA Ops:
  0.7 3.0 collective-permute-start.2
  18.9 13.0 %self_fwd.2 = (bf16[3,1024,64]{2,1,0:T(8,128)(2,1)S(1)}, bf16[3,1024,64]{2,1,0:T(8,128)(2,1)S(1)}, bf16[3,1024,64]{2,1,0:T(8,128)(2,1)S(1)}, bf16[1024,192]{1,0:...) custom-call(s32[4]{0:T(128)S(1)} %compare_select_fusion.1.win, bf16[1024,768]{1,0:T(8,128)(2,1)} %fusion.2.n_ref, ...), custom_call_target="tpu_custom_call" | custom-call | flops 6000000000 | bytes 10000000 | tf_op jit(solution)/shard_map/self_fwd/pallas_call | solution.py:114
  36.9 13.4 %self_fwd.3 = (bf16[3,1024,64]{2,1,0:T(8,128)(2,1)S(1)}, bf16[3,1024,64]{2,1,0:T(8,128)(2,1)S(1)}, bf16[3,1024,64]{2,1,0:T(8,128)(2,1)S(1)}, bf16[1024,192]{1,0:...) custom-call(s32[4]{0:T(128)S(1)} %compare_select_fusion.1.win, bf16[1024,768]{1,0:T(8,128)(2,1)} %fusion.2.n_ref, ...), custom_call_target="tpu_custom_call" | custom-call | flops 6000000000 | bytes 10000000 | tf_op jit(solution)/shard_map/self_fwd/pallas_call | solution.py:114
  50.4 5.2 %add.349 = f32[1024,768]{1,0:T(8,128)} add(f32[1024,768]{1,0:T(8,128)S(1)} %copy-done.69, f32[1024,768]{1,0:T(8,128)} %get-tuple-element.54) | non-fusion elementwise | flops 786432 | bytes 9437184 | tf_op jit(solution)/shard_map/add | solution.py:512
  58.8 2.9 collective-permute-done.4
  65.0 19.5 %collective-permute-done.5.w_ref = bf16[768,768]{1,0:T(8,128)(2,1)S(1)} collective-permute-done((bf16[768,768]{1,0:T(8,128)(2,1)S(1)}, bf16[768,768]{1,0:T(8,128)(2,1)S(1)}, u32[]{:S(2)}, u32[]{:S(2)}) %collective-permute-start.5) | collective-permute-done | bytes 1179680 | tf_op jit(solution)/shard_map/ppermute | solution.py:425
  86.0 3.9 multiply_reduce_fusion.7
  91.6 5.9 %cross_fwd.2 = (bf16[3,1024,64]{2,1,0:T(8,128)(2,1)S(1)}, bf16[1024,192]{1,0:T(8,128)(2,1)S(1)}, f32[1024,8]{1,0:T(8,128)S(1)}, f32[1024,768]{1,0:T(8,128)S(1)}) custom-call(s32[2,4]{1,0:T(2,128)S(1)} %pad_add_fusion.win, bf16[1024,768]{1,0:T(8,128)(2,1)S(1)} %multiply_convert_fusion.1.n_ref, bf16[768,768]{1,0:T(8,128)(2,1)S(1)} %pad_maximum_fusion.3.w_ref, ...), custom_call_target="tpu_custom_call" | custom-call | flops 3000000000 | bytes 8000000 | tf_op jit(solution)/shard_map/cross_fwd/pallas_call | solution.py:265
  100.0 5.9 %cross_fwd.3 = (bf16[3,1024,64]{2,1,0:T(8,128)(2,1)S(1)}, bf16[1024,192]{1,0:T(8,128)(2,1)S(1)}, f32[1024,8]{1,0:T(8,128)S(1)}, f32[1024,768]{1,0:T(8,128)S(1)}) custom-call(s32[2,4]{1,0:T(2,128)S(1)} %pad_add_fusion.win, bf16[1024,768]{1,0:T(8,128)(2,1)S(1)} %multiply_convert_fusion.1.n_ref, bf16[768,768]{1,0:T(8,128)(2,1)S(1)} %copy-done.6, ...), custom_call_target="tpu_custom_call" | custom-call | flops 3000000000 | bytes 8000000 | tf_op jit(solution)/shard_map/cross_fwd/pallas_call | solution.py:265
  108.8 36.4 %collective-permute-done.7 = bf16[2,768,512]{2,1,0:T(8,128)(2,1)} collective-permute-done((bf16[2,768,512]{2,1,0:T(8,128)(2,1)S(1)}, bf16[2,768,512]{2,1,0:T(8,128)(2,1)}, u32[]{:S(2)}, u32[]{:S(2)}) %collective-permute-start.7) | collective-permute-done | bytes 1572896 | tf_op jit(solution)/shard_map/ppermute | solution.py:425
  147.4 16.9 %collective-permute-done.8 = bf16[512,768]{1,0:T(8,128)(2,1)} collective-permute-done((bf16[512,768]{1,0:T(8,128)(2,1)}, bf16[512,768]{1,0:T(8,128)(2,1)}, u32[]{:S(2)}, u32[]{:S(2)}) %collective-permute-start.8) | collective-permute-done | bytes 786464 | tf_op jit(solution)/shard_map/ppermute | solution.py:425
  164.3 3.2 fusion.79
  167.6 3.6 multiply_reduce_fusion.6
  177.8 4.0 fusion.16
  183.8 3.0 convolution_convert_fusion
  189.1 4.8 multiply_convert_fusion.3
  201.6 3.0 convolution_convert_fusion.1
  207.6 5.4 %collective-permute-start.46 = (bf16[256,768]{1,0:T(8,128)(2,1)S(1)}, bf16[256,768]{1,0:T(8,128)(2,1)S(1)}, u32[]{:S(2)}, u32[]{:S(2)}) collective-permute-start(bf16[256,768]{1,0:T(8,128)(2,1)S(1)} %dynamic-slice_bitcast_fusion.3), channel_id=1, source_target_pairs={{0,4},{4,0},{8,12},{12,8},{16,20},{20,16},{24,28},{28,24},{1,5},{5... | collective-permute-start | bytes 1179656 | tf_op jit(solution)/shard_map/ppermute | solution.py:429
  216.2 3.8 collective-permute-done.46
  222.3 16.2 %collective-permute-done.38 = bf16[1536,512]{1,0:T(8,128)(2,1)S(1)} collective-permute-done((bf16[1536,512]{1,0:T(8,128)(2,1)S(1)}, bf16[1536,512]{1,0:T(8,128)(2,1)S(1)}, u32[]{:S(2)}, u32[]{:S(2)}) %collective-permute-start.38) | collective-permute-done | bytes 1572896 | tf_op jit(solution)/shard_map/ppermute | solution.py:425
  239.1 5.7 %collective-permute-start.39 = (bf16[768,512]{1,0:T(8,128)(2,1)S(1)}, bf16[768,512]{1,0:T(8,128)(2,1)S(1)}, u32[]{:S(2)}, u32[]{:S(2)}) collective-permute-start(bf16[768,512]{1,0:T(8,128)(2,1)S(1)} %dynamic-slice_bitcast_fusion), channel_id=1, source_target_pairs={{0,4},{4,0},{8,12},{12,8},{16,20},{20,16},{24,28},{28,24},{1,5},{5... | collective-permute-start | bytes 2359304 | tf_op jit(solution)/shard_map/ppermute | solution.py:429
  247.3 2.9 collective-permute-start.48
  250.4 3.5 collective-permute-done.48
  256.1 4.2 collective-permute-done.39
  264.1 5.1 %fusion.83 = (bf16[1024,768]{1,0:T(8,128)(2,1)S(1)}, f32[1024,768]{1,0:T(8,128)}) fusion(f32[1024]{0:T(1024)S(1)} %broadcast_multiply_fusion.3, f32[1024,768]{1,0:T(8,128)S(1)} %get-tuple-element.117, f32[1024]{0:T(1024)S(1)} %get-tuple-element.156, f32[768]{0:T(1024)S(1)} %copy-done.86, f32[1024,768]{1,0:T(8,128)S(1)} %add_add_fusion, ...), kind=kLoop, calls=%fused_computation.264 | loop fusion | flops 14155776 | bytes 15744001 | tf_op jit(solution)/shard_map/convert_element_type | solution.py:543
  269.3 8.9 %cross_bwd.3 = (bf16[768,768]{1,0:T(8,128)(2,1)S(1)}, f32[1024,768]{1,0:T(8,128)S(1)}, f32[512,768]{1,0:T(8,128)S(1)}) custom-call(s32[2,4]{1,0:T(2,128)S(1)} %pad_add_fusion.win, bf16[1024,768]{1,0:T(8,128)(2,1)S(1)} %get-tuple-element.114.b_ref, bf16[1024,768]{1,0:T(8,128)(2,1)S(1)} %multiply_convert_fusion.1.n_ref, ...), custom_call_target="tpu_custom_call" | custom-call | flops 8000000000 | bytes 12000000 | tf_op jit(solution)/shard_map/cross_bwd/pallas_call | solution.py:323
  281.4 3.5 collective-permute-start.41
  284.9 9.3 %cross_bwd.2 = (bf16[768,768]{1,0:T(8,128)(2,1)S(1)}, f32[1024,768]{1,0:T(8,128)S(1)}, f32[512,768]{1,0:T(8,128)S(1)}) custom-call(s32[2,4]{1,0:T(2,128)S(1)} %pad_add_fusion.win, bf16[1024,768]{1,0:T(8,128)(2,1)S(1)} %get-tuple-element.114.b_ref, bf16[1024,768]{1,0:T(8,128)(2,1)S(1)} %multiply_convert_fusion.1.n_ref, ...), custom_call_target="tpu_custom_call" | custom-call | flops 8000000000 | bytes 12000000 | tf_op jit(solution)/shard_map/cross_bwd/pallas_call | solution.py:323
  294.7 8.1 %collective-permute-done.27 = bf16[768,768]{1,0:T(8,128)(2,1)S(1)} collective-permute-done((bf16[768,768]{1,0:T(8,128)(2,1)S(1)}, bf16[768,768]{1,0:T(8,128)(2,1)S(1)}, u32[]{:S(2)}, u32[]{:S(2)}) %collective-permute-start.27) | collective-permute-done | bytes 1179680 | tf_op jit(solution)/shard_map/ppermute | solution.py:425
  304.9 4.2 collective-permute-start.42
  310.4 4.6 collective-permute-done.42
  319.8 5.8 %collective-permute-done.43 = bf16[384,512]{1,0:T(8,128)(2,1)S(1)} collective-permute-done((bf16[384,512]{1,0:T(8,128)(2,1)S(1)}, bf16[384,512]{1,0:T(8,128)(2,1)S(1)}, u32[]{:S(2)}, u32[]{:S(2)}) %collective-permute-start.43) | collective-permute-done | bytes 393248 | tf_op jit(solution)/shard_map/ppermute | solution.py:429
  331.8 8.0 %collective-permute-done.30 = bf16[96,768]{1,0:T(8,128)(2,1)S(1)} collective-permute-done((bf16[96,768]{1,0:T(8,128)(2,1)S(1)}, bf16[96,768]{1,0:T(8,128)(2,1)S(1)}, u32[]{:S(2)}, u32[]{:S(2)}) %collective-permute-start.30) | collective-permute-done | bytes 147488 | tf_op jit(solution)/shard_map/ppermute | solution.py:429
  340.9 5.9 %collective-permute-done.31 = bf16[96,768]{1,0:T(8,128)(2,1)S(1)} collective-permute-done((bf16[96,768]{1,0:T(8,128)(2,1)S(1)}, bf16[96,768]{1,0:T(8,128)(2,1)S(1)}, u32[]{:S(2)}, u32[]{:S(2)}) %collective-permute-start.31) | collective-permute-done | bytes 147488 | tf_op jit(solution)/shard_map/ppermute | solution.py:429
  347.8 5.9 %collective-permute-done.32 = bf16[192,768]{1,0:T(8,128)(2,1)S(1)} collective-permute-done((bf16[192,768]{1,0:T(8,128)(2,1)S(1)}, bf16[192,768]{1,0:T(8,128)(2,1)S(1)}, u32[]{:S(2)}, u32[]{:S(2)}) %collective-permute-start.32) | collective-permute-done | bytes 294944 | tf_op jit(solution)/shard_map/ppermute | solution.py:429
  356.7 3.0 fusion.82
  360.0 16.8 %self_bwd.3 = (bf16[768,768]{1,0:T(8,128)(2,1)S(1)}, f32[1024,768]{1,0:T(8,128)}, f32[3,1024]{1,0:T(4,128)S(1)}) custom-call(s32[4]{0:T(128)S(1)} %compare_select_fusion.1.win, bf16[1024,768]{1,0:T(8,128)(2,1)} %get-tuple-element.112.b_ref, bf16[1024,768]{1,0:T(8,128)(2,1)} %fusion.2.n_ref, bf16[768,768]{1,0:T(8,128)(2,1)} %collective-permute-done.1.w_ref, ...), custom_call_target="tpu_custom_call" | custom-call | flops 14000000000 | bytes 12000000 | tf_op jit(solution)/shard_map/self_bwd/pallas_call | solution.py:206
  378.9 16.6 %self_bwd.2 = (bf16[768,768]{1,0:T(8,128)(2,1)S(1)}, f32[1024,768]{1,0:T(8,128)}, f32[3,1024]{1,0:T(4,128)S(1)}) custom-call(s32[4]{0:T(128)S(1)} %compare_select_fusion.1.win, bf16[1024,768]{1,0:T(8,128)(2,1)} %get-tuple-element.112.b_ref, bf16[1024,768]{1,0:T(8,128)(2,1)} %fusion.2.n_ref, bf16[768,768]{1,0:T(8,128)(2,1)} %copy-done, ...), custom_call_target="tpu_custom_call" | custom-call | flops 14000000000 | bytes 12000000 | tf_op jit(solution)/shard_map/self_bwd/pallas_call | solution.py:206
  404.6 3.2 add.382
  408.8 5.2 %collective-permute-start.37 = (f32[3,1024]{1,0:T(4,128)S(1)}, f32[3,1024]{1,0:T(4,128)S(1)}, u32[]{:S(2)}, u32[]{:S(2)}) collective-permute-start(f32[3,1024]{1,0:T(4,128)S(1)} %add.410), channel_id=1, source_target_pairs={{0,16},{4,20},{8,24},{12,28},{16,0},{20,4},{24,8},{28,12},{1,17},{... | collective-permute-start | bytes 36872 | tf_op jit(solution)/shard_map/ppermute | solution.py:429
  424.0 14.1 %collective-permute-done.21 = bf16[384,768]{1,0:T(8,128)(2,1)S(1)} collective-permute-done((bf16[384,768]{1,0:T(8,128)(2,1)S(1)}, bf16[384,768]{1,0:T(8,128)(2,1)S(1)}, u32[]{:S(2)}, u32[]{:S(2)}) %collective-permute-start.21) | collective-permute-done | bytes 589856 | tf_op jit(solution)/shard_map/ppermute | solution.py:429
  439.4 7.1 %collective-permute-done.22 = bf16[192,768]{1,0:T(8,128)(2,1)S(1)} collective-permute-done((bf16[192,768]{1,0:T(8,128)(2,1)S(1)}, bf16[192,768]{1,0:T(8,128)(2,1)S(1)}, u32[]{:S(2)}, u32[]{:S(2)}) %collective-permute-start.22) | collective-permute-done | bytes 294944 | tf_op jit(solution)/shard_map/ppermute | solution.py:429
  449.4 5.4 %collective-permute-done.23 = bf16[96,768]{1,0:T(8,128)(2,1)S(1)} collective-permute-done((bf16[96,768]{1,0:T(8,128)(2,1)S(1)}, bf16[96,768]{1,0:T(8,128)(2,1)S(1)}, u32[]{:S(2)}, u32[]{:S(2)}) %collective-permute-start.23) | collective-permute-done | bytes 147488 | tf_op jit(solution)/shard_map/ppermute | solution.py:429
  456.3 5.5 %collective-permute-done.24 = bf16[96,768]{1,0:T(8,128)(2,1)S(1)} collective-permute-done((bf16[96,768]{1,0:T(8,128)(2,1)S(1)}, bf16[96,768]{1,0:T(8,128)(2,1)S(1)}, u32[]{:S(2)}, u32[]{:S(2)}) %collective-permute-start.24) | collective-permute-done | bytes 147488 | tf_op jit(solution)/shard_map/ppermute | solution.py:429
  465.0 5.4 %collective-permute-done.25 = bf16[192,768]{1,0:T(8,128)(2,1)} collective-permute-done((bf16[192,768]{1,0:T(8,128)(2,1)S(1)}, bf16[192,768]{1,0:T(8,128)(2,1)}, u32[]{:S(2)}, u32[]{:S(2)}) %collective-permute-start.25) | collective-permute-done | bytes 294944 | tf_op jit(solution)/shard_map/ppermute | solution.py:429
  477.1 3.0 fusion.20
  482.1 3.5 collective-permute-done.26
  501.6 2.9 collective-permute-done.53
  (458 shorter events, 151.6 us)
Async XLA Ops:
  0.7 15.7 %collective-permute-start.2 = (f32[32,3]{0,1:T(4,128)}, f32[32,3]{0,1:T(4,128)S(1)}, u32[]{:S(2)}, u32[]{:S(2)}) collective-permute-start(f32[32,3]{0,1:T(4,128)} %param.28), channel_id=1, source_target_pairs={{0,2},{1,3},{2,0},{3,1},{4,6},{5,7},{6,4},{7,5},{8,10},{9,11},{10,... | collective-permute-start | bytes 1160 | tf_op jit(solution)/shard_map/ppermute | solution.py:425
  3.7 12.9 %collective-permute-start = (bf16[512,768]{1,0:T(8,128)(2,1)}, bf16[512,768]{1,0:T(8,128)(2,1)S(1)}, u32[]{:S(2)}, u32[]{:S(2)}) collective-permute-start(bf16[512,768]{1,0:T(8,128)(2,1)} %param.21), channel_id=1, source_target_pairs={{0,1},{1,0},{2,3},{3,2},{4,5},{5,4},{6,7},{7,6},{8,9},{9,8},{10,11... | collective-permute-start | bytes 2359304 | tf_op jit(solution)/shard_map/ppermute | solution.py:421
  8.3 28.6 %collective-permute-start.1 = (bf16[768,768]{1,0:T(8,128)(2,1)S(1)}, bf16[768,768]{1,0:T(8,128)(2,1)}, u32[]{:S(2)}, u32[]{:S(2)}) collective-permute-start(bf16[768,768]{1,0:T(8,128)(2,1)S(1)} %pad_maximum_fusion.2.w_ref), channel_id=1, source_target_pairs={{0,2},{1,3},{2,0},{3,1},{4,6},{5,7},{6,4},{7,5},{8,10},{9,11},{10,... | collective-permute-start | bytes 3538952 | tf_op jit(solution)/shard_map/ppermute | solution.py:425
  55.6 30.4 %collective-permute-start.3 = (f32[1024,768]{1,0:T(8,128)}, f32[1024,768]{1,0:T(8,128)}, u32[]{:S(2)}, u32[]{:S(2)}) collective-permute-start(f32[1024,768]{1,0:T(8,128)} %add.349), channel_id=1, source_target_pairs={{0,1},{1,0},{2,3},{3,2},{4,5},{5,4},{6,7},{7,6},{8,9},{9,8},{10,11... | collective-permute-start | bytes 9437192 | tf_op jit(solution)/shard_map/ppermute | solution.py:421
  56.4 28.0 %collective-permute-start.5 = (bf16[768,768]{1,0:T(8,128)(2,1)S(1)}, bf16[768,768]{1,0:T(8,128)(2,1)S(1)}, u32[]{:S(2)}, u32[]{:S(2)}) collective-permute-start(bf16[768,768]{1,0:T(8,128)(2,1)S(1)} %pad_maximum_fusion.3.w_ref), channel_id=1, source_target_pairs={{0,2},{1,3},{2,0},{3,1},{4,6},{5,7},{6,4},{7,5},{8,10},{9,11},{10,... | collective-permute-start | bytes 3538952 | tf_op jit(solution)/shard_map/ppermute | solution.py:425
  108.2 59.3 %collective-permute-start.6 = (f32[1024,768]{1,0:T(8,128)}, f32[1024,768]{1,0:T(8,128)}, u32[]{:S(2)}, u32[]{:S(2)}) collective-permute-start(f32[1024,768]{1,0:T(8,128)} %add.359), channel_id=1, source_target_pairs={{0,1},{1,0},{2,3},{3,2},{4,5},{5,4},{6,7},{7,6},{8,9},{9,8},{10,11... | collective-permute-start | bytes 9437192 | tf_op jit(solution)/shard_map/ppermute | solution.py:421
  108.6 36.6 %collective-permute-start.7 = (bf16[2,768,512]{2,1,0:T(8,128)(2,1)S(1)}, bf16[2,768,512]{2,1,0:T(8,128)(2,1)}, u32[]{:S(2)}, u32[]{:S(2)}) collective-permute-start(bf16[2,768,512]{2,1,0:T(8,128)(2,1)S(1)} %copy-done.72), channel_id=1, source_target_pairs={{0,2},{1,3},{2,0},{3,1},{4,6},{5,7},{6,4},{7,5},{8,10},{9,11},{10,... | collective-permute-start | bytes 4718600 | tf_op jit(solution)/shard_map/ppermute | solution.py:425
  108.6 38.8 %collective-permute-start.10 = (bf16[512,768]{1,0:T(8,128)(2,1)}, bf16[512,768]{1,0:T(8,128)(2,1)}, u32[]{:S(2)}, u32[]{:S(2)}) collective-permute-start(bf16[512,768]{1,0:T(8,128)(2,1)} %param.23), channel_id=1, source_target_pairs={{0,1},{1,0},{2,3},{3,2},{4,5},{5,4},{6,7},{7,6},{8,9},{9,8},{10,11... | collective-permute-start | bytes 2359304 | tf_op jit(solution)/shard_map/ppermute | solution.py:421
  145.2 19.1 %collective-permute-start.8 = (bf16[512,768]{1,0:T(8,128)(2,1)}, bf16[512,768]{1,0:T(8,128)(2,1)}, u32[]{:S(2)}, u32[]{:S(2)}) collective-permute-start(bf16[512,768]{1,0:T(8,128)(2,1)} %param.30), channel_id=1, source_target_pairs={{0,2},{1,3},{2,0},{3,1},{4,6},{5,7},{6,4},{7,5},{8,10},{9,11},{10,... | collective-permute-start | bytes 2359304 | tf_op jit(solution)/shard_map/ppermute | solution.py:425
  186.9 20.5 %collective-permute-start.45 = (bf16[512,768]{1,0:T(8,128)(2,1)S(1)}, bf16[512,768]{1,0:T(8,128)(2,1)S(1)}, u32[]{:S(2)}, u32[]{:S(2)}) collective-permute-start(bf16[512,768]{1,0:T(8,128)(2,1)S(1)} %convolution_convert_fusion), channel_id=1, source_target_pairs={{0,2},{1,3},{2,0},{3,1},{4,6},{5,7},{6,4},{7,5},{8,10},{9,11},{10,... | collective-permute-start | bytes 2359304 | tf_op jit(solution)/shard_map/ppermute | solution.py:425
  187.6 50.9 %collective-permute-start.38 = (bf16[1536,512]{1,0:T(8,128)(2,1)S(1)}, bf16[1536,512]{1,0:T(8,128)(2,1)S(1)}, u32[]{:S(2)}, u32[]{:S(2)}) collective-permute-start(bf16[1536,512]{1,0:T(8,128)(2,1)S(1)} %pad_maximum_fusion.1), channel_id=1, source_target_pairs={{0,2},{1,3},{2,0},{3,1},{4,6},{5,7},{6,4},{7,5},{8,10},{9,11},{10,... | collective-permute-start | bytes 4718600 | tf_op jit(solution)/shard_map/ppermute | solution.py:425
  200.5 62.4 %collective-permute-start.11 = (f32[1024,768]{1,0:T(8,128)S(1)}, f32[1024,768]{1,0:T(8,128)S(1)}, u32[]{:S(2)}, u32[]{:S(2)}) collective-permute-start(f32[1024,768]{1,0:T(8,128)S(1)} %add_add_fusion), channel_id=1, source_target_pairs={{0,1},{1,0},{2,3},{3,2},{4,5},{5,4},{6,7},{7,6},{8,9},{9,8},{10,11... | collective-permute-start | bytes 9437192 | tf_op jit(solution)/shard_map/ppermute | solution.py:421
  207.6 12.3 %collective-permute-start.46 = (bf16[256,768]{1,0:T(8,128)(2,1)S(1)}, bf16[256,768]{1,0:T(8,128)(2,1)S(1)}, u32[]{:S(2)}, u32[]{:S(2)}) collective-permute-start(bf16[256,768]{1,0:T(8,128)(2,1)S(1)} %dynamic-slice_bitcast_fusion.3), channel_id=1, source_target_pairs={{0,4},{4,0},{8,12},{12,8},{16,20},{20,16},{24,28},{28,24},{1,5},{5... | collective-permute-start | bytes 1179656 | tf_op jit(solution)/shard_map/ppermute | solution.py:429
  220.1 27.0 %collective-permute-start.47 = (bf16[128,768]{1,0:T(8,128)(2,1)S(1)}, bf16[128,768]{1,0:T(8,128)(2,1)S(1)}, u32[]{:S(2)}, u32[]{:S(2)}) collective-permute-start(bf16[128,768]{1,0:T(8,128)(2,1)S(1)} %dynamic-slice_bitcast_fusion.7), channel_id=1, source_target_pairs={{0,8},{4,12},{8,0},{12,4},{16,24},{20,28},{24,16},{28,20},{1,9},{5... | collective-permute-start | bytes 589832 | tf_op jit(solution)/shard_map/ppermute | solution.py:429
  239.1 21.3 %collective-permute-start.39 = (bf16[768,512]{1,0:T(8,128)(2,1)S(1)}, bf16[768,512]{1,0:T(8,128)(2,1)S(1)}, u32[]{:S(2)}, u32[]{:S(2)}) collective-permute-start(bf16[768,512]{1,0:T(8,128)(2,1)S(1)} %dynamic-slice_bitcast_fusion), channel_id=1, source_target_pairs={{0,4},{4,0},{8,12},{12,8},{16,20},{20,16},{24,28},{28,24},{1,5},{5... | collective-permute-start | bytes 2359304 | tf_op jit(solution)/shard_map/ppermute | solution.py:429
  247.3 6.6 %collective-permute-start.48 = (bf16[64,768]{1,0:T(8,128)(2,1)S(1)}, bf16[64,768]{1,0:T(8,128)(2,1)S(1)}, u32[]{:S(2)}, u32[]{:S(2)}) collective-permute-start(bf16[64,768]{1,0:T(8,128)(2,1)S(1)} %dynamic-slice_bitcast_fusion.11), channel_id=1, source_target_pairs={{0,16},{4,20},{8,24},{12,28},{16,0},{20,4},{24,8},{28,12},{1,17},{... | collective-permute-start | bytes 294920 | tf_op jit(solution)/shard_map/ppermute | solution.py:429
  250.3 58.9 %collective-permute-start.9 = (f32[512,768]{1,0:T(8,128)S(1)}, f32[512,768]{1,0:T(8,128)S(1)}, u32[]{:S(2)}, u32[]{:S(2)}) collective-permute-start(f32[512,768]{1,0:T(8,128)S(1)} %constant_dynamic-slice_fusion.2), channel_id=1, source_target_pairs={{0,1},{1,0},{2,3},{3,2},{4,5},{5,4},{6,7},{7,6},{8,9},{9,8},{10,11... | collective-permute-start | bytes 4718600 | tf_op jit(solution)/shard_map/ppermute | solution.py:421
  253.9 24.4 %collective-permute-start.49 = (bf16[64,768]{1,0:T(8,128)(2,1)S(1)}, bf16[64,768]{1,0:T(8,128)(2,1)S(1)}, u32[]{:S(2)}, u32[]{:S(2)}) collective-permute-start(bf16[64,768]{1,0:T(8,128)(2,1)S(1)} %fusion.63), channel_id=1, source_target_pairs={{0,16},{4,20},{8,24},{12,28},{16,0},{20,4},{24,8},{28,12},{1,17},{... | collective-permute-start | bytes 294920 | tf_op jit(solution)/shard_map/ppermute | solution.py:429
  260.7 19.9 %collective-permute-start.40 = (bf16[384,512]{1,0:T(8,128)(2,1)S(1)}, bf16[384,512]{1,0:T(8,128)(2,1)S(1)}, u32[]{:S(2)}, u32[]{:S(2)}) collective-permute-start(bf16[384,512]{1,0:T(8,128)(2,1)S(1)} %dynamic-slice_bitcast_fusion.4), channel_id=1, source_target_pairs={{0,8},{4,12},{8,0},{12,4},{16,24},{20,28},{24,16},{28,20},{1,9},{5... | collective-permute-start | bytes 1179656 | tf_op jit(solution)/shard_map/ppermute | solution.py:429
  278.2 24.6 %collective-permute-start.27 = (bf16[768,768]{1,0:T(8,128)(2,1)S(1)}, bf16[768,768]{1,0:T(8,128)(2,1)S(1)}, u32[]{:S(2)}, u32[]{:S(2)}) collective-permute-start(bf16[768,768]{1,0:T(8,128)(2,1)S(1)} %get-tuple-element.89), channel_id=1, source_target_pairs={{0,2},{1,3},{2,0},{3,1},{4,6},{5,7},{6,4},{7,5},{8,10},{9,11},{10,... | collective-permute-start | bytes 3538952 | tf_op jit(solution)/shard_map/ppermute | solution.py:425
  278.3 39.2 %collective-permute-start.50 = (bf16[128,768]{1,0:T(8,128)(2,1)S(1)}, bf16[128,768]{1,0:T(8,128)(2,1)}, u32[]{:S(2)}, u32[]{:S(2)}) collective-permute-start(bf16[128,768]{1,0:T(8,128)(2,1)S(1)} %maximum_select_fusion.14), channel_id=1, source_target_pairs={{0,8},{4,12},{8,0},{12,4},{16,24},{20,28},{24,16},{28,20},{1,9},{5... | collective-permute-start | bytes 589832 | tf_op jit(solution)/shard_map/ppermute | solution.py:429
  281.4 22.5 %collective-permute-start.41 = (bf16[192,512]{1,0:T(8,128)(2,1)}, bf16[192,512]{1,0:T(8,128)(2,1)}, u32[]{:S(2)}, u32[]{:S(2)}) collective-permute-start(bf16[192,512]{1,0:T(8,128)(2,1)} %dynamic-slice_bitcast_fusion.8), channel_id=1, source_target_pairs={{0,16},{4,20},{8,24},{12,28},{16,0},{20,4},{24,8},{28,12},{1,17},{... | collective-permute-start | bytes 589832 | tf_op jit(solution)/shard_map/ppermute | solution.py:429
  294.6 60.1 %collective-permute-start.12 = (f32[1024,768]{1,0:T(8,128)S(1)}, f32[1024,768]{1,0:T(8,128)S(1)}, u32[]{:S(2)}, u32[]{:S(2)}) collective-permute-start(f32[1024,768]{1,0:T(8,128)S(1)} %add.377), channel_id=1, source_target_pairs={{0,1},{1,0},{2,3},{3,2},{4,5},{5,4},{6,7},{7,6},{8,9},{9,8},{10,11... | collective-permute-start | bytes 9437192 | tf_op jit(solution)/shard_map/ppermute | solution.py:421
  303.1 12.1 %collective-permute-start.28 = (bf16[384,768]{1,0:T(8,128)(2,1)S(1)}, bf16[384,768]{1,0:T(8,128)(2,1)S(1)}, u32[]{:S(2)}, u32[]{:S(2)}) collective-permute-start(bf16[384,768]{1,0:T(8,128)(2,1)S(1)} %dynamic-slice_bitcast_fusion.1), channel_id=1, source_target_pairs={{0,4},{4,0},{8,12},{12,8},{16,20},{20,16},{24,28},{28,24},{1,5},{5... | collective-permute-start | bytes 1769480 | tf_op jit(solution)/shard_map/ppermute | solution.py:429
  304.9 10.1 %collective-permute-start.42 = (bf16[192,512]{1,0:T(8,128)(2,1)S(1)}, bf16[192,512]{1,0:T(8,128)(2,1)S(1)}, u32[]{:S(2)}, u32[]{:S(2)}) collective-permute-start(bf16[192,512]{1,0:T(8,128)(2,1)S(1)} %fusion.58), channel_id=1, source_target_pairs={{0,16},{4,20},{8,24},{12,28},{16,0},{20,4},{24,8},{28,12},{1,17},{... | collective-permute-start | bytes 589832 | tf_op jit(solution)/shard_map/ppermute | solution.py:429
  315.1 10.4 %collective-permute-start.43 = (bf16[384,512]{1,0:T(8,128)(2,1)S(1)}, bf16[384,512]{1,0:T(8,128)(2,1)S(1)}, u32[]{:S(2)}, u32[]{:S(2)}) collective-permute-start(bf16[384,512]{1,0:T(8,128)(2,1)S(1)} %maximum_select_fusion.10), channel_id=1, source_target_pairs={{0,8},{4,12},{8,0},{12,4},{16,24},{20,28},{24,16},{28,20},{1,9},{5... | collective-permute-start | bytes 1179656 | tf_op jit(solution)/shard_map/ppermute | solution.py:429
  315.4 14.1 %collective-permute-start.29 = (bf16[192,768]{1,0:T(8,128)(2,1)S(1)}, bf16[192,768]{1,0:T(8,128)(2,1)S(1)}, u32[]{:S(2)}, u32[]{:S(2)}) collective-permute-start(bf16[192,768]{1,0:T(8,128)(2,1)S(1)} %dynamic-slice_bitcast_fusion.5), channel_id=1, source_target_pairs={{0,8},{4,12},{8,0},{12,4},{16,24},{20,28},{24,16},{28,20},{1,9},{5... | collective-permute-start | bytes 884744 | tf_op jit(solution)/shard_map/ppermute | solution.py:429
  318.6 11.1 %collective-permute-start.51 = (bf16[256,768]{1,0:T(8,128)(2,1)S(1)}, bf16[256,768]{1,0:T(8,128)(2,1)S(1)}, u32[]{:S(2)}, u32[]{:S(2)}) collective-permute-start(bf16[256,768]{1,0:T(8,128)(2,1)S(1)} %maximum_select_fusion.11), channel_id=1, source_target_pairs={{0,4},{4,0},{8,12},{12,8},{16,20},{20,16},{24,28},{28,24},{1,5},{5... | collective-permute-start | bytes 1179656 | tf_op jit(solution)/shard_map/ppermute | solution.py:429
  319.7 20.2 %collective-permute-start.14 = (f32[256,768]{1,0:T(8,128)S(1)}, f32[256,768]{1,0:T(8,128)S(1)}, u32[]{:S(2)}, u32[]{:S(2)}) collective-permute-start(f32[256,768]{1,0:T(8,128)S(1)} %constant_dynamic-slice_fusion), channel_id=1, source_target_pairs={{0,1},{1,0},{2,3},{3,2},{4,5},{5,4},{6,7},{7,6},{8,9},{9,8},{10,11... | collective-permute-start | bytes 2359304 | tf_op jit(solution)/shard_map/ppermute | solution.py:421
  325.9 21.0 %collective-permute-start.44 = (bf16[768,512]{1,0:T(8,128)(2,1)S(1)}, bf16[768,512]{1,0:T(8,128)(2,1)S(1)}, u32[]{:S(2)}, u32[]{:S(2)}) collective-permute-start(bf16[768,512]{1,0:T(8,128)(2,1)S(1)} %maximum_select_fusion.6), channel_id=1, source_target_pairs={{0,4},{4,0},{8,12},{12,8},{16,20},{20,16},{24,28},{28,24},{1,5},{5... | collective-permute-start | bytes 2359304 | tf_op jit(solution)/shard_map/ppermute | solution.py:429
  329.6 10.1 %collective-permute-start.30 = (bf16[96,768]{1,0:T(8,128)(2,1)S(1)}, bf16[96,768]{1,0:T(8,128)(2,1)S(1)}, u32[]{:S(2)}, u32[]{:S(2)}) collective-permute-start(bf16[96,768]{1,0:T(8,128)(2,1)S(1)} %dynamic-slice_bitcast_fusion.9), channel_id=1, source_target_pairs={{0,16},{4,20},{8,24},{12,28},{16,0},{20,4},{24,8},{28,12},{1,17},{... | collective-permute-start | bytes 442376 | tf_op jit(solution)/shard_map/ppermute | solution.py:429
  339.8 7.0 %collective-permute-start.31 = (bf16[96,768]{1,0:T(8,128)(2,1)S(1)}, bf16[96,768]{1,0:T(8,128)(2,1)S(1)}, u32[]{:S(2)}, u32[]{:S(2)}) collective-permute-start(bf16[96,768]{1,0:T(8,128)(2,1)S(1)} %fusion.59), channel_id=1, source_target_pairs={{0,16},{4,20},{8,24},{12,28},{16,0},{20,4},{24,8},{28,12},{1,17},{... | collective-permute-start | bytes 442376 | tf_op jit(solution)/shard_map/ppermute | solution.py:429
  346.9 6.8 %collective-permute-start.32 = (bf16[192,768]{1,0:T(8,128)(2,1)S(1)}, bf16[192,768]{1,0:T(8,128)(2,1)S(1)}, u32[]{:S(2)}, u32[]{:S(2)}) collective-permute-start(bf16[192,768]{1,0:T(8,128)(2,1)S(1)} %maximum_select_fusion.13), channel_id=1, source_target_pairs={{0,8},{4,12},{8,0},{12,4},{16,24},{20,28},{24,16},{28,20},{1,9},{5... | collective-permute-start | bytes 884744 | tf_op jit(solution)/shard_map/ppermute | solution.py:429
  353.9 63.0 %collective-permute-start.33 = (bf16[384,768]{1,0:T(8,128)(2,1)S(1)}, bf16[384,768]{1,0:T(8,128)(2,1)S(1)}, u32[]{:S(2)}, u32[]{:S(2)}) collective-permute-start(bf16[384,768]{1,0:T(8,128)(2,1)S(1)} %maximum_select_fusion.9), channel_id=1, source_target_pairs={{0,4},{4,0},{8,12},{12,8},{16,20},{20,16},{24,28},{28,24},{1,5},{5... | collective-permute-start | bytes 1769480 | tf_op jit(solution)/shard_map/ppermute | solution.py:429
  376.8 18.7 %collective-permute-start.34 = (f32[3,1024]{1,0:T(4,128)S(1)}, f32[3,1024]{1,0:T(4,128)S(1)}, u32[]{:S(2)}, u32[]{:S(2)}) collective-permute-start(f32[3,1024]{1,0:T(4,128)S(1)} %get-tuple-element.91), channel_id=1, source_target_pairs={{0,2},{1,3},{2,0},{3,1},{4,6},{5,7},{6,4},{7,5},{8,10},{9,11},{10,... | collective-permute-start | bytes 36872 | tf_op jit(solution)/shard_map/ppermute | solution.py:425
  376.8 44.2 %collective-permute-start.20 = (bf16[768,768]{1,0:T(8,128)(2,1)S(1)}, bf16[768,768]{1,0:T(8,128)(2,1)}, u32[]{:S(2)}, u32[]{:S(2)}) collective-permute-start(bf16[768,768]{1,0:T(8,128)(2,1)S(1)} %get-tuple-element.87), channel_id=1, source_target_pairs={{0,2},{1,3},{2,0},{3,1},{4,6},{5,7},{6,4},{7,5},{8,10},{9,11},{10,... | collective-permute-start | bytes 3538952 | tf_op jit(solution)/shard_map/ppermute | solution.py:425
  400.7 7.2 %collective-permute-start.36 = (f32[3,1024]{1,0:T(4,128)}, f32[3,1024]{1,0:T(4,128)}, u32[]{:S(2)}, u32[]{:S(2)}) collective-permute-start(f32[3,1024]{1,0:T(4,128)} %add.409), channel_id=1, source_target_pairs={{0,8},{4,12},{8,0},{12,4},{16,24},{20,28},{24,16},{28,20},{1,9},{5... | collective-permute-start | bytes 36872 | tf_op jit(solution)/shard_map/ppermute | solution.py:429
  408.8 7.0 %collective-permute-start.37 = (f32[3,1024]{1,0:T(4,128)S(1)}, f32[3,1024]{1,0:T(4,128)S(1)}, u32[]{:S(2)}, u32[]{:S(2)}) collective-permute-start(f32[3,1024]{1,0:T(4,128)S(1)} %add.410), channel_id=1, source_target_pairs={{0,16},{4,20},{8,24},{12,28},{16,0},{20,4},{24,8},{28,12},{1,17},{... | collective-permute-start | bytes 36872 | tf_op jit(solution)/shard_map/ppermute | solution.py:429
  415.3 31.4 %collective-permute-start.13 = (f32[512,768]{1,0:T(8,128)}, f32[512,768]{1,0:T(8,128)}, u32[]{:S(2)}, u32[]{:S(2)}) collective-permute-start(f32[512,768]{1,0:T(8,128)} %constant_dynamic-slice_fusion.1), channel_id=1, source_target_pairs={{0,1},{1,0},{2,3},{3,2},{4,5},{5,4},{6,7},{7,6},{8,9},{9,8},{10,11... | collective-permute-start | bytes 4718600 | tf_op jit(solution)/shard_map/ppermute | solution.py:421
  422.7 15.4 %collective-permute-start.21 = (bf16[384,768]{1,0:T(8,128)(2,1)S(1)}, bf16[384,768]{1,0:T(8,128)(2,1)S(1)}, u32[]{:S(2)}, u32[]{:S(2)}) collective-permute-start(bf16[384,768]{1,0:T(8,128)(2,1)S(1)} %dynamic-slice_bitcast_fusion.2), channel_id=1, source_target_pairs={{0,4},{4,0},{8,12},{12,8},{16,20},{20,16},{24,28},{28,24},{1,5},{5... | collective-permute-start | bytes 1769480 | tf_op jit(solution)/shard_map/ppermute | solution.py:429
  438.3 8.2 %collective-permute-start.22 = (bf16[192,768]{1,0:T(8,128)(2,1)S(1)}, bf16[192,768]{1,0:T(8,128)(2,1)S(1)}, u32[]{:S(2)}, u32[]{:S(2)}) collective-permute-start(bf16[192,768]{1,0:T(8,128)(2,1)S(1)} %dynamic-slice_bitcast_fusion.6), channel_id=1, source_target_pairs={{0,8},{4,12},{8,0},{12,4},{16,24},{20,28},{24,16},{28,20},{1,9},{5... | collective-permute-start | bytes 884744 | tf_op jit(solution)/shard_map/ppermute | solution.py:429
  446.6 8.2 %collective-permute-start.23 = (bf16[96,768]{1,0:T(8,128)(2,1)S(1)}, bf16[96,768]{1,0:T(8,128)(2,1)S(1)}, u32[]{:S(2)}, u32[]{:S(2)}) collective-permute-start(bf16[96,768]{1,0:T(8,128)(2,1)S(1)} %dynamic-slice_bitcast_fusion.10), channel_id=1, source_target_pairs={{0,16},{4,20},{8,24},{12,28},{16,0},{20,4},{24,8},{28,12},{1,17},{... | collective-permute-start | bytes 442376 | tf_op jit(solution)/shard_map/ppermute | solution.py:429
  449.4 6.2 %collective-permute-start.15 = (f32[768]{0:T(1024)S(1)}, f32[768]{0:T(1024)S(1)}, u32[]{:S(2)}, u32[]{:S(2)}) collective-permute-start(f32[768]{0:T(1024)S(1)} %get-tuple-element.96), channel_id=1, source_target_pairs={{0,1},{1,0},{2,3},{3,2},{4,5},{5,4},{6,7},{7,6},{8,9},{9,8},{10,11... | collective-permute-start | bytes 9224 | tf_op jit(solution)/shard_map/ppermute | solution.py:421
  454.8 7.0 %collective-permute-start.24 = (bf16[96,768]{1,0:T(8,128)(2,1)S(1)}, bf16[96,768]{1,0:T(8,128)(2,1)S(1)}, u32[]{:S(2)}, u32[]{:S(2)}) collective-permute-start(bf16[96,768]{1,0:T(8,128)(2,1)S(1)} %fusion.60), channel_id=1, source_target_pairs={{0,16},{4,20},{8,24},{12,28},{16,0},{20,4},{24,8},{28,12},{1,17},{... | collective-permute-start | bytes 442376 | tf_op jit(solution)/shard_map/ppermute | solution.py:429
  455.6 8.8 %collective-permute-start.16 = (f32[3,768]{1,0:T(4,128)S(1)}, f32[3,768]{1,0:T(4,128)S(1)}, u32[]{:S(2)}, u32[]{:S(2)}) collective-permute-start(f32[3,768]{1,0:T(4,128)S(1)} %pad_maximum_fusion.6), channel_id=1, source_target_pairs={{0,2},{1,3},{2,0},{3,1},{4,6},{5,7},{6,4},{7,5},{8,10},{9,11},{10,... | collective-permute-start | bytes 27656 | tf_op jit(solution)/shard_map/ppermute | solution.py:425
  461.9 8.5 %collective-permute-start.25 = (bf16[192,768]{1,0:T(8,128)(2,1)S(1)}, bf16[192,768]{1,0:T(8,128)(2,1)}, u32[]{:S(2)}, u32[]{:S(2)}) collective-permute-start(bf16[192,768]{1,0:T(8,128)(2,1)S(1)} %maximum_select_fusion.12), channel_id=1, source_target_pairs={{0,8},{4,12},{8,0},{12,4},{16,24},{20,28},{24,16},{28,20},{1,9},{5... | collective-permute-start | bytes 884744 | tf_op jit(solution)/shard_map/ppermute | solution.py:429
  464.5 7.9 %collective-permute-start.17 = (f32[3,768]{1,0:T(4,128)S(1)}, f32[3,768]{1,0:T(4,128)S(1)}, u32[]{:S(2)}, u32[]{:S(2)}) collective-permute-start(f32[3,768]{1,0:T(4,128)S(1)} %fusion.76), channel_id=1, source_target_pairs={{0,4},{4,0},{8,12},{12,8},{16,20},{20,16},{24,28},{28,24},{1,5},{5... | collective-permute-start | bytes 27656 | tf_op jit(solution)/shard_map/ppermute | solution.py:429
  471.8 13.8 %collective-permute-start.26 = (bf16[384,768]{1,0:T(8,128)(2,1)S(1)}, bf16[384,768]{1,0:T(8,128)(2,1)S(1)}, u32[]{:S(2)}, u32[]{:S(2)}) collective-permute-start(bf16[384,768]{1,0:T(8,128)(2,1)S(1)} %maximum_select_fusion.8), channel_id=1, source_target_pairs={{0,4},{4,0},{8,12},{12,8},{16,20},{20,16},{24,28},{28,24},{1,5},{5... | collective-permute-start | bytes 1769480 | tf_op jit(solution)/shard_map/ppermute | solution.py:429
  (119 other events, 930.2 us)
